TPU v7x, 32 devices: a whole 2x2x4 slice. The times are simulated.
32 devices in a mesh: rep: 4 (over y, core), fsdp: 8 (over z, x).
Axes of the slice: x: 2, y: 2, z: 4, core: 2. Of those that a mesh axis runs over, the one named last changes fastest.
Arguments:
- token_ids: int32 [32, 128], P(('rep', 'fsdp')), may hold values from 0 to 30527
- lengths: int32 [32], P(('rep', 'fsdp')), may hold values from 1 to 128, 2048 in all
- slot_order: int32 [32], replicated, may hold values from 0 to 31, each once
- pair_labels: int32 [32], replicated, may hold values from 0 to 31, as said below
- embedding: float32 [30528, 768], P('fsdp'), may hold values from -0.21875 to 0.21875
- attend_weight: float32 [768, 2304], P('fsdp'), may hold values from -0.21875 to 0.21875
- attention_output_matrix: float32 [768, 768], P('fsdp'), may hold values from -1.25 to 1.25
- gate_up: float32 [768, 6144], P('fsdp'), may hold values from -0.21875 to 0.21875
- contract_kernel: float32 [3072, 768], P('fsdp'), may hold values from -0.109375 to 0.109375
- norm_params: float32 [6, 768], P(None, 'fsdp'), may hold values from -0.3 to 1.4, as said below
- embedding_first: float32 [30528, 768], P('fsdp'), may hold values from -2.3841858e-06 to 2.3841858e-06
- embedding_second: float32 [30528, 768], P('fsdp'), may hold values from 1.0135626e-14 to 4.0542504e-14
- attend_first: float32 [768, 2304], P('fsdp'), may hold values from -2.3841858e-06 to 2.3841858e-06
- attend_second: float32 [768, 2304], P('fsdp'), may hold values from 1.0135626e-14 to 4.0542504e-14
- output_first: float32 [768, 768], P('fsdp'), may hold values from -2.3841858e-06 to 2.3841858e-06
- output_second: float32 [768, 768], P('fsdp'), may hold values from 1.0135626e-14 to 4.0542504e-14
- gate_up_first: float32 [768, 6144], P('fsdp'), may hold values from -2.3841858e-06 to 2.3841858e-06
- gate_up_second: float32 [768, 6144], P('fsdp'), may hold values from 1.0135626e-14 to 4.0542504e-14
- down_first: float32 [3072, 768], P('fsdp'), may hold values from -2.3841858e-06 to 2.3841858e-06
- down_second: float32 [3072, 768], P('fsdp'), may hold values from 1.0135626e-14 to 4.0542504e-14
- norm_first: float32 [6, 768], P(None, 'fsdp'), may hold values from -2.670288e-05 to 2.670288e-05
- norm_second: float32 [6, 768], P(None, 'fsdp'), may hold values from 1.0135626e-12 to 4.0542504e-12
Outputs:
- loss_value: float32 [], replicated
- grad_norm: float32 [], replicated
- embedding_next: float32 [30528, 768], P('fsdp')
- embedding_first_next: float32 [30528, 768], P('fsdp')
- embedding_second_next: float32 [30528, 768], P('fsdp')
- attend_next: float32 [768, 2304], P('fsdp')
- attend_first_next: float32 [768, 2304], P('fsdp')
- attend_second_next: float32 [768, 2304], P('fsdp')
- output_next: float32 [768, 768], P('fsdp')
- output_first_next: float32 [768, 768], P('fsdp')
- output_second_next: float32 [768, 768], P('fsdp')
- gate_up_next: float32 [768, 6144], P('fsdp')
- gate_up_first_next: float32 [768, 6144], P('fsdp')
- gate_up_second_next: float32 [768, 6144], P('fsdp')
- down_next: float32 [3072, 768], P('fsdp')
- down_first_next: float32 [3072, 768], P('fsdp')
- down_second_next: float32 [3072, 768], P('fsdp')
- norm_next: float32 [6, 768], P(None, 'fsdp')
- norm_first_next: float32 [6, 768], P(None, 'fsdp')
- norm_second_next: float32 [6, 768], P(None, 'fsdp')
Inputs may be any that keep to these rules, and one draw needn't show every extreme that they name: pair_labels[pair_labels[i]] = i and pair_labels[i] != i: the 32 sequences form disjoint pairs. Slot s holds the sequence whose index in the given order is slot_order[s]; each index once. `lengths`: the longest sequence has exactly 128 tokens. `norm_params`: rows 0, 2 and 4 are gains, rows 1, 3 and 5 the matching shifts.
All inputs are finite; a program needn't handle non-finite values. No bound on the sum of `lengths` on one device may be relied on, other than what follows from the above.
Results may differ from a plain program's by a relative error of at most 0.011.
The roundings to bfloat16 on the way count: a program that leaves them out, or rounds other values in their place, can miss the bound.
Values may be sent and summed in bfloat16 or wider, within the bound.
A program may use at most 152 MiB of HBM per device.

v0:
```python
import jax
import jax.numpy as jnp
from jax import lax
from jax.sharding import PartitionSpec as P

H = 12
HD = 64
FF = 3072
STEP = 4


exact_arithmetic_mode = lax.Precision.HIGHEST
logit_divisor = 0.05
clip_level = 0.001
learn_rate = 0.02
norm_rate = 0.3
weight_decay = 0.01
beta_first = 0.5
beta_second = 0.75
adam_floor = 1e-08


def layer_norm(values, gain, shift):
    centred = values - jnp.mean(values, axis=-1, keepdims=True)
    inverse = lax.rsqrt(jnp.mean(centred * centred, axis=-1, keepdims=True) + 1e-06)
    normed = centred * inverse
    return (normed * gain + shift, normed, inverse)


def norm_back(upstream, normed, inverse, gain):
    scaled = upstream * gain
    inner = (
        scaled
        - jnp.mean(scaled, axis=-1, keepdims=True)
        - normed * jnp.mean(scaled * normed, axis=-1, keepdims=True)
    )
    return (inner * inverse, jnp.sum(upstream * normed, axis=0), jnp.sum(upstream, axis=0))


def rotary(seq_len, head_size):
    position = jnp.arange(seq_len).astype(jnp.float32)
    frequency = 1000.0 ** (-2.0 * jnp.arange(head_size // 2).astype(jnp.float32) / head_size)
    angles = position[:, None] * frequency[None, :]
    return (jnp.cos(angles)[:, None, :], jnp.sin(angles)[:, None, :])


def rotate(values, cosine_table, sine_table):
    middle = values.shape[-1] // 2
    lower_half, upper_half = (values[..., :middle], values[..., middle:])
    return jnp.concatenate(
        [
            lower_half * cosine_table - upper_half * sine_table,
            upper_half * cosine_table + lower_half * sine_table,
        ],
        axis=-1,
    )


def rotate_back(incoming_gradient, cosine_table, sine_table):
    middle = incoming_gradient.shape[-1] // 2
    lower_half, upper_half = (incoming_gradient[..., :middle], incoming_gradient[..., middle:])
    return jnp.concatenate(
        [
            lower_half * cosine_table + upper_half * sine_table,
            upper_half * cosine_table - lower_half * sine_table,
        ],
        axis=-1,
    )


def contrast(pooled, pair_labels):
    amount = pooled.shape[0]
    main_trace_entries = jnp.arange(amount)[:, None] == jnp.arange(amount)[None, :]
    summed = 0.0
    for feature_column in (pooled.shape[1] // 12, pooled.shape[1] // 3, pooled.shape[1]):
        portion = pooled[:, :feature_column]
        unit_length_embeddings = portion * lax.rsqrt(
            jnp.sum(portion * portion, axis=1, keepdims=True) + 1e-06
        )
        cosine_logit_table = (
            jnp.dot(
                unit_length_embeddings, unit_length_embeddings.T, precision=exact_arithmetic_mode
            )
            / logit_divisor
        )
        cosine_logit_table = jnp.where(main_trace_entries, -1000000000.0, cosine_logit_table)
        row_max = jnp.max(cosine_logit_table, axis=1, keepdims=True)
        log_total = row_max[:, 0] + jnp.log(jnp.sum(jnp.exp(cosine_logit_table - row_max), axis=1))
        target = jnp.take_along_axis(cosine_logit_table, pair_labels[:, None], axis=1)[:, 0]
        summed = summed + jnp.mean(log_total - target)
    return summed / 3.0


def regroup(values, groups, group_size):
    return values.reshape(values.shape[0], groups, group_size, values.shape[2]).transpose(
        1, 0, 2, 3
    )


def attend_block(query, keys, received_entries, key_mask):
    scaling = query.shape[-1] ** (-0.5)
    scores = jnp.einsum("qhd,khd->hqk", query, keys, preferred_element_type=jnp.float32) * scaling
    scores = jnp.where(key_mask, scores, -1000000000.0)
    row_max = jnp.max(scores, axis=-1, keepdims=True)
    raised = jnp.exp(scores - row_max)
    summed = jnp.sum(raised, axis=-1, keepdims=True)
    chances = (raised / summed).astype(jnp.bfloat16)
    result = jnp.einsum(
        "hqk,khd->qhd", chances, received_entries, preferred_element_type=jnp.float32
    )
    return (result, row_max[..., 0] + jnp.log(summed[..., 0]))


def attend_back(query, keys, received_entries, grad_out, log_total, key_mask):
    scaling = query.shape[-1] ** (-0.5)
    scores = jnp.einsum("qhd,khd->hqk", query, keys, preferred_element_type=jnp.float32) * scaling
    scores = jnp.where(key_mask, scores, -1000000000.0)
    chances = jnp.exp(scores - log_total[..., None])
    d_values = jnp.einsum(
        "hqk,qhd->khd", chances.astype(jnp.bfloat16), grad_out, preferred_element_type=jnp.float32
    )
    d_chances = jnp.einsum(
        "qhd,khd->hqk", grad_out, received_entries, preferred_element_type=jnp.float32
    )
    pairwise_inner_product = jnp.sum(chances * d_chances, axis=-1, keepdims=True)
    d_scores = (chances * (d_chances - pairwise_inner_product)).astype(jnp.bfloat16)
    d_query = (
        jnp.einsum("hqk,khd->qhd", d_scores, keys, preferred_element_type=jnp.float32) * scaling
    )
    d_keys = (
        jnp.einsum("hqk,qhd->khd", d_scores, query, preferred_element_type=jnp.float32) * scaling
    )
    return (d_query, d_keys, d_values)


def attention(query, keys, received_entries, key_mask, length, block_size):
    seq_len, head_count, head_size = query.shape
    group_size = min(4, head_count)
    groups = head_count // group_size
    query_g = regroup(query, groups, group_size)
    keys_g = regroup(keys, groups, group_size)
    values_g = regroup(received_entries, groups, group_size)

    def one_block(block_index):
        offset = block_index * block_size

        def compute(unused):
            return lax.map(
                lambda items: attend_block(items[0], items[1], items[2], key_mask),
                (query_g, keys_g, values_g),
            )

        def skipped(unused):
            return (
                jnp.zeros((groups, block_size, group_size, head_size), jnp.float32),
                jnp.zeros((groups, group_size, block_size), jnp.float32),
            )

        return lax.cond(offset < length, compute, skipped, 0)

    results, log_totals = lax.map(one_block, jnp.arange(seq_len // block_size))
    return (results.transpose(0, 2, 1, 3, 4).reshape(seq_len, head_count * head_size), log_totals)


def attention_back(
    query, keys, received_entries, grad_out, key_mask, length, block_size, log_totals
):
    seq_len, head_count, head_size = query.shape
    group_size = min(4, head_count)
    groups = head_count // group_size
    query_g = regroup(query, groups, group_size)
    keys_g = regroup(keys, groups, group_size)
    values_g = regroup(received_entries, groups, group_size)
    grad_g = regroup(grad_out, groups, group_size)
    zero_state = jnp.zeros(keys_g.shape, jnp.float32)

    def one_block(running, block_index):
        offset = block_index * block_size

        def compute(state):
            d_query, d_keys, d_values = lax.map(
                lambda items: attend_back(
                    items[0], items[1], items[2], items[3], items[4], key_mask
                ),
                (query_g, keys_g, values_g, grad_g, log_totals[block_index]),
            )
            return ((state[0] + d_keys, state[1] + d_values), d_query)

        def skipped(state):
            return (state, jnp.zeros((groups, block_size, group_size, head_size), jnp.float32))

        return lax.cond(offset < length, compute, skipped, running)

    (d_keys, d_values), d_query = lax.scan(
        one_block, (zero_state, zero_state), jnp.arange(seq_len // block_size)
    )
    return (
        d_query.transpose(0, 2, 1, 3, 4).reshape(seq_len, head_count, head_size),
        d_keys.transpose(1, 0, 2, 3).reshape(seq_len, head_count, head_size),
        d_values.transpose(1, 0, 2, 3).reshape(seq_len, head_count, head_size),
    )


def adamw_step(weight, grad, first, second, rate):
    first_new = beta_first * first + (1.0 - beta_first) * grad
    second_new = beta_second * second + (1.0 - beta_second) * grad * grad
    first_fix = 1.0 - beta_first**STEP
    second_fix = 1.0 - beta_second**STEP
    update = first_new / first_fix / (jnp.sqrt(second_new / second_fix) + adam_floor)
    return (weight - rate * (update + weight_decay * weight), first_new, second_new)


def local(
    token_ids,
    lengths,
    slot_order,
    pair_labels,
    embedding,
    attend_weight,
    attention_output_matrix,
    gate_up,
    contract_kernel,
    norm_params,
    embedding_first,
    embedding_second,
    attend_first,
    attend_second,
    output_first,
    output_second,
    gate_up_first,
    gate_up_second,
    down_first,
    down_second,
    norm_first,
    norm_second,
):
    token_list = token_ids[0]
    length = lengths[0]
    seq_len = token_list.shape[0]
    feature_column = embedding.shape[1]
    block_size = min(512, seq_len)
    positions = jnp.arange(seq_len)
    key_mask = positions < length
    present = key_mask.astype(jnp.float32)
    length_float = length.astype(jnp.float32)
    members = (
        attend_weight.astype(jnp.bfloat16),
        attention_output_matrix.astype(jnp.bfloat16),
        gate_up.astype(jnp.bfloat16),
        contract_kernel.astype(jnp.bfloat16),
        norm_params.astype(jnp.bfloat16),
    )
    w_attend, w_output, w_gateup, w_down, gain_low = (
        lax.all_gather(members[0], "fsdp", axis=0, tiled=True),
        lax.all_gather(members[1], "fsdp", axis=0, tiled=True),
        lax.all_gather(members[2], "fsdp", axis=0, tiled=True),
        lax.all_gather(members[3], "fsdp", axis=0, tiled=True),
        lax.all_gather(members[4], "fsdp", axis=1, tiled=True),
    )
    gain_rows = gain_low.astype(jnp.float32)
    table_part = embedding.astype(jnp.bfloat16)
    shard_rows = embedding.shape[0]
    shard_start = lax.axis_index("fsdp") * shard_rows
    group_tokens = lax.all_gather(token_ids, "fsdp", axis=0, tiled=True).reshape(-1)
    wanted = group_tokens - shard_start
    inside = (wanted >= 0) & (wanted < shard_rows)
    fetched = jnp.take(table_part, jnp.clip(wanted, 0, shard_rows - 1), axis=0).astype(jnp.float32)
    embedded = lax.psum_scatter(
        jnp.where(inside[:, None], fetched, 0.0).astype(jnp.bfloat16),
        "fsdp",
        scatter_dimension=0,
        tiled=True,
    ).astype(jnp.float32)
    normed_zero, hat_zero, inv_zero = layer_norm(embedded, gain_rows[0], gain_rows[1])
    zero_low = normed_zero.astype(jnp.bfloat16)
    projected = jnp.dot(zero_low, w_attend, preferred_element_type=jnp.float32)
    cosine_table, sine_table = rotary(seq_len, HD)
    query_low = rotate(
        projected[:, :feature_column].reshape(seq_len, H, HD), cosine_table, sine_table
    ).astype(jnp.bfloat16)
    keys_low = rotate(
        projected[:, feature_column : 2 * feature_column].reshape(seq_len, H, HD),
        cosine_table,
        sine_table,
    ).astype(jnp.bfloat16)
    values_low = projected[:, 2 * feature_column :].reshape(seq_len, H, HD).astype(jnp.bfloat16)
    attended, log_totals = attention(query_low, keys_low, values_low, key_mask, length, block_size)
    attended_low = attended.astype(jnp.bfloat16)
    branch = jnp.dot(attended_low, w_output, preferred_element_type=jnp.float32)
    normed_one, hat_one, inv_one = layer_norm(normed_zero + branch, gain_rows[2], gain_rows[3])
    one_low = normed_one.astype(jnp.bfloat16)
    gate_all = jnp.dot(one_low, w_gateup, preferred_element_type=jnp.float32)
    gate_part, up_part = (gate_all[:, :FF], gate_all[:, FF:])
    logistic = jax.nn.sigmoid(gate_part)
    swished = gate_part * logistic
    mixed_low = (swished * up_part).astype(jnp.bfloat16)
    feed = jnp.dot(mixed_low, w_down, preferred_element_type=jnp.float32)
    normed_two, hat_two, inv_two = layer_norm(normed_one + feed, gain_rows[4], gain_rows[5])
    pooled = jnp.sum(normed_two * present[:, None], axis=0) / length_float
    everyone = lax.all_gather(pooled[None, :], ("rep", "fsdp"), axis=0, tiled=True)
    given = jnp.zeros_like(everyone).at[slot_order].set(everyone)
    loss_value, pullback = jax.vjp(lambda values: contrast(values, pair_labels), given)
    d_given = pullback(jnp.ones((), jnp.float32))[0]
    d_mine = lax.dynamic_index_in_dim(
        d_given[slot_order], lax.axis_index(("rep", "fsdp")), 0, keepdims=False
    )
    w_attend, w_output, w_gateup, w_down, gain_low = (
        lax.all_gather(members[0], "fsdp", axis=0, tiled=True),
        lax.all_gather(members[1], "fsdp", axis=0, tiled=True),
        lax.all_gather(members[2], "fsdp", axis=0, tiled=True),
        lax.all_gather(members[3], "fsdp", axis=0, tiled=True),
        lax.all_gather(members[4], "fsdp", axis=1, tiled=True),
    )
    gain_rows = gain_low.astype(jnp.float32)
    d_two = d_mine[None, :] * present[:, None] / length_float
    d_sum_two, d_gain_two, d_shift_two = norm_back(d_two, hat_two, inv_two, gain_rows[4])
    d_feed = d_sum_two.astype(jnp.bfloat16)
    grad_down = jnp.einsum("lf,ld->fd", mixed_low, d_feed, preferred_element_type=jnp.float32)
    d_mixed = jnp.einsum("ld,fd->lf", d_feed, w_down, preferred_element_type=jnp.float32)
    swish_slope = logistic * (1.0 + gate_part * (1.0 - logistic))
    d_gateall = jnp.concatenate(
        [d_mixed * up_part * swish_slope, d_mixed * swished], axis=-1
    ).astype(jnp.bfloat16)
    grad_gateup = jnp.einsum("ld,lf->df", one_low, d_gateall, preferred_element_type=jnp.float32)
    d_one = d_sum_two + jnp.einsum(
        "lf,df->ld", d_gateall, w_gateup, preferred_element_type=jnp.float32
    )
    d_sum_one, d_gain_one, shift_one_gradient = norm_back(d_one, hat_one, inv_one, gain_rows[2])
    d_branch = d_sum_one.astype(jnp.bfloat16)
    grad_output = jnp.einsum(
        "ld,le->de", attended_low, d_branch, preferred_element_type=jnp.float32
    )
    d_attended = jnp.einsum("le,de->ld", d_branch, w_output, preferred_element_type=jnp.float32)
    d_attended = d_attended.astype(jnp.bfloat16).reshape(seq_len, H, HD)
    d_query, d_keys, d_values = attention_back(
        query_low, keys_low, values_low, d_attended, key_mask, length, block_size, log_totals
    )
    d_query = rotate_back(d_query, cosine_table, sine_table).reshape(seq_len, feature_column)
    d_keys = rotate_back(d_keys, cosine_table, sine_table).reshape(seq_len, feature_column)
    d_projected = jnp.concatenate(
        [d_query, d_keys, d_values.reshape(seq_len, feature_column)], axis=-1
    ).astype(jnp.bfloat16)
    grad_attend = jnp.einsum("ld,le->de", zero_low, d_projected, preferred_element_type=jnp.float32)
    d_zero = d_sum_one + jnp.einsum(
        "le,de->ld", d_projected, w_attend, preferred_element_type=jnp.float32
    )
    d_embedded, d_gain_zero, d_shift_zero = norm_back(d_zero, hat_zero, inv_zero, gain_rows[0])
    grad_norms = jnp.stack(
        [d_gain_zero, d_shift_zero, d_gain_one, shift_one_gradient, d_gain_two, d_shift_two]
    )
    shard_grads = (
        lax.psum_scatter(grad_attend, "fsdp", scatter_dimension=0, tiled=True),
        lax.psum_scatter(grad_output, "fsdp", scatter_dimension=0, tiled=True),
        lax.psum_scatter(grad_gateup, "fsdp", scatter_dimension=0, tiled=True),
        lax.psum_scatter(grad_down, "fsdp", scatter_dimension=0, tiled=True),
        lax.psum_scatter(grad_norms, "fsdp", scatter_dimension=1, tiled=True),
    )
    group_grads = lax.all_gather(d_embedded, "fsdp", axis=0, tiled=True)
    within = group_tokens - shard_start
    inside = (within >= 0) & (within < shard_rows)
    segment = jnp.where(inside, within, shard_rows)
    grad_table = jax.ops.segment_sum(group_grads, segment, num_segments=shard_rows + 1)[:shard_rows]
    summed_grads = lax.psum(
        (
            grad_table,
            shard_grads[0],
            shard_grads[1],
            shard_grads[2],
            shard_grads[3],
            shard_grads[4],
        ),
        "rep",
    )
    squares = jnp.sum(summed_grads[0] * summed_grads[0])
    for member in summed_grads[1:]:
        squares = squares + jnp.sum(member * member)
    grad_norm = jnp.sqrt(lax.psum(squares, "fsdp"))
    factor = jnp.minimum(1.0, clip_level / (grad_norm + 1e-06))
    emb_next = adamw_step(
        embedding, summed_grads[0] * factor, embedding_first, embedding_second, learn_rate
    )
    att_next = adamw_step(
        attend_weight, summed_grads[1] * factor, attend_first, attend_second, learn_rate
    )
    out_next = adamw_step(
        attention_output_matrix, summed_grads[2] * factor, output_first, output_second, learn_rate
    )
    gate_next = adamw_step(
        gate_up, summed_grads[3] * factor, gate_up_first, gate_up_second, learn_rate
    )
    down_next = adamw_step(
        contract_kernel, summed_grads[4] * factor, down_first, down_second, learn_rate
    )
    norm_next = adamw_step(
        norm_params, summed_grads[5] * factor, norm_first, norm_second, norm_rate
    )
    return (
        loss_value,
        grad_norm,
        emb_next[0],
        emb_next[1],
        emb_next[2],
        att_next[0],
        att_next[1],
        att_next[2],
        out_next[0],
        out_next[1],
        out_next[2],
        gate_next[0],
        gate_next[1],
        gate_next[2],
        down_next[0],
        down_next[1],
        down_next[2],
        norm_next[0],
        norm_next[1],
        norm_next[2],
    )


def solution(mesh):
    in_specs = (
        P(("rep", "fsdp"), None),
        P(("rep", "fsdp")),
        P(),
        P(),
        P("fsdp", None),
        P("fsdp", None),
        P("fsdp", None),
        P("fsdp", None),
        P("fsdp", None),
        P(None, "fsdp"),
        P("fsdp", None),
        P("fsdp", None),
        P("fsdp", None),
        P("fsdp", None),
        P("fsdp", None),
        P("fsdp", None),
        P("fsdp", None),
        P("fsdp", None),
        P("fsdp", None),
        P("fsdp", None),
        P(None, "fsdp"),
        P(None, "fsdp"),
    )
    out_specs = (
        P(),
        P(),
        P("fsdp", None),
        P("fsdp", None),
        P("fsdp", None),
        P("fsdp", None),
        P("fsdp", None),
        P("fsdp", None),
        P("fsdp", None),
        P("fsdp", None),
        P("fsdp", None),
        P("fsdp", None),
        P("fsdp", None),
        P("fsdp", None),
        P("fsdp", None),
        P("fsdp", None),
        P("fsdp", None),
        P(None, "fsdp"),
        P(None, "fsdp"),
        P(None, "fsdp"),
    )
    return jax.shard_map(local, mesh=mesh, in_specs=in_specs, out_specs=out_specs, check_vma=False)
```

profile of v0, /device:TPU:0, one launch (start us, length us, event | category | flops | bytes accessed | tf_op | source)
XLA Modules:
  0.0 1745.9 jit_solution(11971243870419030813)
XLA Ops:
  7.2 7.5 convert_element_type.180
  14.7 22.1 %all-gather.1 = s32[8,1,128]{2,1,0:T(1,128)S(1)} all-gather(s32[1,1,128]{2,1,0:T(1,128)S(1)} %bitcast.257), channel_id=1, replica_groups=mesh['rep'=4,'fsdp'=8] {'fsdp'}, dimensions={0}, use_global_device_ids=true | all-gather | bytes 4608 | tf_op jit(solution)/shard_map/all_gather | solution.py:264
  37.5 7.9 gather_fusion
  51.9 26.0 %all-gather.2 = bf16[8,96,6]{1,2,0:T(8,128)(2,1)S(1)} all-gather(bf16[1,96,6]{1,2,0:T(8,128)(2,1)S(1)} %convert_bitcast_fusion), channel_id=1, replica_groups=mesh['rep'=4,'fsdp'=8] {'fsdp'}, dimensions={0}, use_global_device_ids=true | all-gather | bytes 10368 | tf_op jit(solution)/shard_map/all_gather | solution.py:258
  80.5 28.9 %reduce-scatter.9.cloned.1.call-done = bf16[128,768]{1,0:T(8,128)(2,1)} async-done(((bf16[1024,768]{1,0:T(8,128)(2,1)}), bf16[128,768]{1,0:T(8,128)(2,1)}) %reduce-scatter.9.cloned.1.call-update) | async-done | bytes 196624 | tf_op jit(solution)/shard_map/reduce_scatter | solution.py:268
  111.6 64.9 %all-gather.10.cloned.1.call-done = bf16[768,2304]{1,0:T(8,128)(2,1)} async-done(((bf16[96,2304]{1,0:T(8,128)(2,1)}), bf16[768,2304]{1,0:T(8,128)(2,1)}) %all-gather.10.cloned.1.call-update) | async-done | bytes 3538960 | tf_op jit(solution)/shard_map/all_gather | solution.py:254
  180.1 5.2 conditional.2
  180.2 5.2 while.29
  185.3 33.8 %all-gather.12.cloned.1.call-done = bf16[768,768]{1,0:T(8,128)(2,1)} async-done(((bf16[96,768]{1,0:T(8,128)(2,1)}), bf16[768,768]{1,0:T(8,128)(2,1)}) %all-gather.12.cloned.1.call-update) | async-done | bytes 1179664 | tf_op jit(solution)/shard_map/all_gather | solution.py:255
  221.2 137.6 %all-gather.14.cloned.1.call-done = bf16[768,6144]{1,0:T(8,128)(2,1)} async-done(((bf16[96,6144]{1,0:T(8,128)(2,1)}), bf16[768,6144]{1,0:T(8,128)(2,1)}) %all-gather.14.cloned.1.call-update) | async-done | bytes 9437200 | tf_op jit(solution)/shard_map/all_gather | solution.py:256
  358.8 5.2 fusion.162
  366.1 73.6 %all-gather.16.cloned.1.call-done = bf16[3072,768]{1,0:T(8,128)(2,1)} async-done(((bf16[384,768]{1,0:T(8,128)(2,1)}), bf16[3072,768]{1,0:T(8,128)(2,1)}) %all-gather.16.cloned.1.call-update) | async-done | bytes 4718608 | tf_op jit(solution)/shard_map/all_gather | solution.py:257
  443.4 65.8 %all-gather.3 = f32[32,1,768]{2,1,0:T(1,128)S(1)} all-gather(f32[1,1,768]{2,1,0:T(1,128)S(1)} %reshape.442), channel_id=2, replica_groups=mesh['rep'=4,'fsdp'=8] {'rep','fsdp'}, dimensions={0}, use_global_device_ids=true | all-gather | bytes 101376 | tf_op jit(solution)/shard_map/all_gather | solution.py:300
  520.7 5.2 multiply_convert_fusion.2
  531.3 13.5 conditional.3
  531.4 11.4 while.30
  559.3 5.3 fusion.79
  566.0 8.0 fusion.52
  575.8 33.3 %all-gather.18.cloned.1.call-done = f32[1024,768]{1,0:T(8,128)} async-done(((f32[128,768]{1,0:T(8,128)}), f32[1024,768]{1,0:T(8,128)}) %all-gather.18.cloned.1.call-update) | async-done | bytes 3145744 | tf_op jit(solution)/shard_map/all_gather | solution.py:358
  609.1 13.2 scatter_custom_fusion.1
  622.3 9.6 slice.129
  631.9 49.4 %reduce-scatter.13.cloned.1.call-done = f32[96,768]{1,0:T(8,128)} async-done(((f32[768,768]{1,0:T(8,128)}), f32[96,768]{1,0:T(8,128)}) %reduce-scatter.13.cloned.1.call-update) | async-done | bytes 294928 | tf_op jit(solution)/shard_map/reduce_scatter | solution.py:353
  681.3 132.8 %reduce-scatter.11.cloned.1.call-done = f32[96,2304]{1,0:T(8,128)} async-done(((f32[768,2304]{1,0:T(8,128)}), f32[96,2304]{1,0:T(8,128)}) %reduce-scatter.11.cloned.1.call-update) | async-done | bytes 884752 | tf_op jit(solution)/shard_map/reduce_scatter | solution.py:352
  814.1 166.7 %reduce-scatter.17.cloned.1.call-done = f32[384,768]{1,0:T(8,128)} async-done(((f32[3072,768]{1,0:T(8,128)}), f32[384,768]{1,0:T(8,128)}) %reduce-scatter.17.cloned.1.call-update) | async-done | bytes 1179664 | tf_op jit(solution)/shard_map/reduce_scatter | solution.py:355
  980.8 315.6 %reduce-scatter.15.cloned.1.call-done = f32[96,6144]{1,0:T(8,128)} async-done(((f32[768,6144]{1,0:T(8,128)}), f32[96,6144]{1,0:T(8,128)}) %reduce-scatter.15.cloned.1.call-update) | async-done | bytes 2359312 | tf_op jit(solution)/shard_map/reduce_scatter | solution.py:354
  1298.4 62.4 %reduce-scatter.19.cloned.1.call-done = f32[96,6]{1,0:T(8,128)} async-done(((f32[768,6]{1,0:T(8,128)}), f32[96,6]{1,0:T(8,128)}) %reduce-scatter.19.cloned.1.call-update) | async-done | bytes 2320
  1361.7 5.6 psum.54
  1368.0 280.8 %all-reduce.5.cloned.1.call-done = (f32[3816,768]{1,0:T(8,128)}, f32[96,2304]{1,0:T(8,128)}, f32[96,768]{1,0:T(8,128)}, f32[96,6144]{1,0:T(8,128)}, f32[384,768]{1,0:T(8,128)}) async-done(((f32[3816,768]{1,0:T(8,128)}, f32[96,2304]{1,0:T(8,128)}, f32[96,768]{1,0:T(8,128)}, f32[96,6144]{1,0:T(8,128)}, f32[384,768]{1,0:T(8,128)}), (f32[3816,768]{1,0:T(8,128)}, f32[96,2304]{1,0:T(8,128)}, f32[96,768]{1,0:T(8,128)}, ...) | async-done | bytes 16441360 | tf_op jit(solution)/shard_map/psum | solution.py:363
  1648.8 8.1 multiply_reduce_fusion.1
  1664.4 22.1 %psum.55 = f32[]{:T(128)} all-reduce(f32[]{:T(128)S(6)} %add.383), channel_id=1, replica_groups=mesh['rep'=4,'fsdp'=8] {'fsdp'}, use_global_device_ids=true, to_apply=%region_71.73 | all-reduce | flops 1 | bytes 8 | tf_op jit(solution)/shard_map/psum | solution.py:377
  1687.2 33.5 %multiply_subtract_fusion = (f32[3816,768]{1,0:T(8,128)}, f32[3816,768]{1,0:T(8,128)}, f32[3816,768]{1,0:T(8,128)}) fusion(f32[3816,768]{1,0:T(8,128)} %param.36, f32[3816,768]{1,0:T(8,128)} %param.42, f32[3816,768]{1,0:T(8,128)} %get-tuple-element.306, f32[]{:T(128)S(6)} %min.25, f32[3816,768]{1,0:T(8,128)} %param.43), kind=kLoop, calls=%fused_computation.64 | loop fusion | flops 43960320 | bytes 82059264 | tf_op jit(solution)/shard_map/sub | solution.py:210
  1727.6 5.2 multiply_subtract_fusion.1
  (325 shorter events, 90.5 us)
Async XLA Ops:
  7.2 102.2 %reduce-scatter.9.cloned.1.call-start = ((), (), s32[]{:S(2)}) async-start(), calls=%async_computation.6 | async-start | bytes 1769472 | tf_op jit(solution)/shard_map/reduce_scatter | solution.py:268
  47.1 129.4 %all-gather.10.cloned.1.call-start = ((), (), s32[]{:S(2)}) async-start(), calls=%async_computation.7 | async-start | bytes 3981312 | tf_op jit(solution)/shard_map/all_gather | solution.py:254
  48.0 171.1 %all-gather.12.cloned.1.call-start = ((), (), s32[]{:S(2)}) async-start(), calls=%async_computation.8 | async-start | bytes 1327104 | tf_op jit(solution)/shard_map/all_gather | solution.py:255
  48.8 310.0 %all-gather.14.cloned.1.call-start = ((), (), s32[]{:S(2)}) async-start(), calls=%async_computation.9 | async-start | bytes 10616832 | tf_op jit(solution)/shard_map/all_gather | solution.py:256
  50.2 28.4 %copy-start.62 = (s32[32]{0:T(128)S(1)}, s32[32]{0:T(128)}, u32[]{:S(2)}) copy-start(s32[32]{0:T(128)} %param.35) | copy-start | bytes 388
  50.2 28.9 %copy-start.65 = (s32[32]{0:T(128)S(1)}, s32[32]{0:T(128)}, u32[]{:S(2)}) copy-start(s32[32]{0:T(128)} %param.34) | copy-start | bytes 388
  50.2 389.5 %all-gather.16.cloned.1.call-start = ((), (), s32[]{:S(2)}) async-start(), calls=%async_computation.10 | async-start | bytes 5308416 | tf_op jit(solution)/shard_map/all_gather | solution.py:257
  51.2 558.0 %all-gather.18.cloned.1.call-start = ((), (), s32[]{:S(2)}) async-start(), calls=%async_computation.11 | async-start | bytes 3538944 | tf_op jit(solution)/shard_map/all_gather | solution.py:358
  78.1 102.1 %copy-start.24 = (pred[128]{0:T(512)(128)(4,1)}, pred[128]{0:T(512)(128)(4,1)S(1)}, u32[]{:S(2)}) copy-start(pred[128]{0:T(512)(128)(4,1)S(1)} %iota_compare_fusion.2) | copy-start | bytes 388
  79.1 97.4 %copy-start.64 = (s32[32]{0:T(128)}, s32[32]{0:T(128)S(1)}, u32[]{:S(2)}) copy-start(s32[32]{0:T(128)S(1)} %compare_select_fusion.3) | copy-start | bytes 388
  110.4 108.7 %copy-start.34 = (f32[128]{0:T(128)}, f32[128]{0:T(128)S(1)}, u32[]{:S(2)}) copy-start(f32[128]{0:T(128)S(1)} %broadcast_multiply_fusion.14) | copy-start | bytes 1540
  111.6 107.5 %copy-start.41 = (f32[128]{0:T(128)}, f32[128]{0:T(128)S(1)}, u32[]{:S(2)}) copy-start(f32[128]{0:T(128)S(1)} %add_rsqrt_fusion.2) | copy-start | bytes 1540
  180.1 39.0 %copy-start.4 = (bf16[128,768]{1,0:T(8,128)(2,1)S(1)}, bf16[128,768]{1,0:T(8,128)(2,1)}, u32[]{:S(2)}) copy-start(bf16[128,768]{1,0:T(8,128)(2,1)} %reduce-scatter.9.cloned.1.call-done) | copy-start | bytes 589828
  221.0 218.8 %copy-start.28 = (f32[128]{0:T(128)}, f32[128]{0:T(128)S(1)}, u32[]{:S(2)}) copy-start(f32[128]{0:T(128)S(1)} %broadcast_multiply_fusion.13) | copy-start | bytes 1540
  221.2 218.6 %copy-start.31 = (f32[128]{0:T(128)}, f32[128]{0:T(128)S(1)}, u32[]{:S(2)}) copy-start(f32[128]{0:T(128)S(1)} %add_rsqrt_fusion.1) | copy-start | bytes 1540
  366.1 77.1 %copy-start.21 = (f32[768]{0:T(1024)S(1)}, f32[768]{0:T(1024)}, u32[]{:S(2)}) copy-start(f32[768]{0:T(1024)} %get-tuple-element.255) | copy-start | bytes 9220
  366.1 77.1 %copy-start.38 = (f32[768]{0:T(1024)S(1)}, f32[768]{0:T(1024)}, u32[]{:S(2)}) copy-start(f32[768]{0:T(1024)} %get-tuple-element.256) | copy-start | bytes 9220
  366.1 77.1 %copy-start.46 = (f32[128]{0:T(128)S(1)}, f32[128]{0:T(128)}, u32[]{:S(2)}) copy-start(f32[128]{0:T(128)} %fusion.157) | copy-start | bytes 1540
  443.0 70.7 %copy-start.63 = (s32[32]{0:T(128)S(1)}, s32[32]{0:T(128)}, u32[]{:S(2)}) copy-start(s32[32]{0:T(128)} %param.35) | copy-start | bytes 388
  443.0 71.4 %copy-start.52 = (s32[32]{0:T(128)S(1)}, s32[32]{0:T(128)}, u32[]{:S(2)}) copy-start(s32[32]{0:T(128)} %get-tuple-element.360) | copy-start | bytes 388
  443.0 72.0 %copy-start.43 = (f32[128]{0:T(128)}, f32[128]{0:T(128)S(1)}, u32[]{:S(2)}) copy-start(f32[128]{0:T(128)S(1)} %broadcast_multiply_fusion.12) | copy-start | bytes 1540
  443.2 71.8 %copy-start.49 = (f32[128]{0:T(128)}, f32[128]{0:T(128)S(1)}, u32[]{:S(2)}) copy-start(f32[128]{0:T(128)S(1)} %add_rsqrt_fusion) | copy-start | bytes 1540
  516.7 9.2 slice-start
  551.5 129.8 %reduce-scatter.13.cloned.1.call-start = ((), (), s32[]{:S(2)}) async-start(), calls=%async_computation.13 | async-start | bytes 2654208 | tf_op jit(solution)/shard_map/reduce_scatter | solution.py:353
  554.4 259.8 %reduce-scatter.11.cloned.1.call-start = ((), (), s32[]{:S(2)}) async-start(), calls=%async_computation.12 | async-start | bytes 7962624 | tf_op jit(solution)/shard_map/reduce_scatter | solution.py:352
  558.7 422.2 %reduce-scatter.17.cloned.1.call-start = ((), (), s32[]{:S(2)}) async-start(), calls=%async_computation.15 | async-start | bytes 10616832 | tf_op jit(solution)/shard_map/reduce_scatter | solution.py:355
  564.7 731.8 %reduce-scatter.15.cloned.1.call-start = ((), (), s32[]{:S(2)}) async-start(), calls=%async_computation.14 | async-start | bytes 21233664 | tf_op jit(solution)/shard_map/reduce_scatter | solution.py:354
  574.0 786.8 %reduce-scatter.19.cloned.1.call-start = ((), (), s32[]{:S(2)}) async-start(), calls=%async_computation.16 | async-start | bytes 442368
  575.8 1073.0 %all-reduce.5.cloned.1.call-start = ((), (), s32[]{:S(2)}) async-start(), calls=%async_computation.17 | async-start | bytes 32882688 | tf_op jit(solution)/shard_map/psum | solution.py:363
  1648.7 8.1 copy-start.9
  1648.7 8.9 copy-start.14
  1648.8 9.6 copy-start.3
  (49 other events, 159.3 us)
Sparse Core Ops, SparseCore 0:
  47.3 62.0 reduce-scatter.8
  112.4 64.1 all-gather.9
  179.5 39.5 all-gather.11
  221.9 136.8 all-gather.13
  361.6 78.0 all-gather.15
  551.6 57.4 all-gather.17
  613.6 67.6 reduce-scatter.12
  686.0 128.0 reduce-scatter.10
  818.3 162.4 reduce-scatter.16
  984.5 311.8 reduce-scatter.14
  1300.3 60.4 reduce-scatter.18
  1364.2 284.4 all-reduce.4
where the time goes:
time: 1750 us
  waiting for transfers between devices  1380 us (79%)
  blocking collectives  142 us (8%)
  other arithmetic  104 us (6%)
  matrix products  61.4 us (4%)
  local copies, waits for them, and re-layouts  33.2 us (2%)
  between operations  25.2 us (1%)
    reduce_scatter x1, waiting for transfers between devices, local(): lax.psum_scatter(grad_gateup, 'fsdp', scatter_dimension=0, tiled=True)  316 us
    psum x1, waiting for transfers between devices, local(): lax.psum((grad_table, shard_grads[0], shard_grads[1], shard_grads[2], sha...  281 us
    reduce_scatter x1, waiting for transfers between devices, local(): lax.psum_scatter(grad_down, 'fsdp', scatter_dimension=0, tiled=True)  167 us
    all_gather x1, waiting for transfers between devices, local(): lax.all_gather(members[2], 'fsdp', axis=0, tiled=True)  138 us
    reduce_scatter x1, waiting for transfers between devices, local(): lax.psum_scatter(grad_attend, 'fsdp', scatter_dimension=0, tiled=True)  133 us
    all_gather x1, waiting for transfers between devices, local(): lax.all_gather(members[3], 'fsdp', axis=0, tiled=True)  73.6 us
    all_gather x1, blocking collectives, local(): lax.all_gather(pooled[None, :], ('rep', 'fsdp'), axis=0, tiled=True)  65.8 us
    all_gather x1, waiting for transfers between devices, local(): lax.all_gather(members[0], 'fsdp', axis=0, tiled=True)  64.9 us
  transfers between devices with their start and end apart: 12, of which 12 were waited for; matrix products, arithmetic and copies ran while one was open for 4% of the time, Pallas kernels for 0%

commit v1 on v0

v1 whole, which is shorter than its diff:
```python
import functools

import jax
import jax.numpy as jnp
from jax import lax
from jax.experimental import pallas as pl
from jax.experimental.pallas import tpu as pltpu
from jax.sharding import PartitionSpec as P

H = 12
HD = 64
STEP = 4
TP = 4
MESH = pl.DeviceIdType.MESH
BF = jnp.bfloat16
F32 = jnp.float32

logit_divisor = 0.05
clip_level = 0.001
learn_rate = 0.02
norm_rate = 0.3
weight_decay = 0.01
beta_first = 0.5
beta_second = 0.75
adam_floor = 1e-08


def dot(a, b):
    return lax.dot_general(a, b, (((1,), (0,)), ((), ())), preferred_element_type=F32)


def dot_nt(a, b):
    return lax.dot_general(a, b, (((1,), (1,)), ((), ())), preferred_element_type=F32)


def dot_tn(a, b):
    return lax.dot_general(a, b, (((0,), (0,)), ((), ())), preferred_element_type=F32)


def layer_norm(values, gain, shift):
    centred = values - jnp.mean(values, axis=-1, keepdims=True)
    inverse = lax.rsqrt(jnp.mean(centred * centred, axis=-1, keepdims=True) + 1e-06)
    normed = centred * inverse
    return normed * gain + shift, normed, inverse


def norm_back(upstream, normed, inverse, gain):
    scaled = upstream * gain
    inner = (
        scaled
        - jnp.mean(scaled, axis=-1, keepdims=True)
        - normed * jnp.mean(scaled * normed, axis=-1, keepdims=True)
    )
    return (
        inner * inverse,
        jnp.sum(upstream * normed, axis=0, keepdims=True),
        jnp.sum(upstream, axis=0, keepdims=True),
    )


def step_kernel(sizes, *refs):
    NR, NF, S, D, rows = sizes
    NX, NZ, NG = 2, NF // 2, NR // TP
    N, nr = NR * NF, D // NF
    HI = lax.Precision.HIGHEST
    (
        ids_in, idcol_in, gn_in, table_in, pieces_in, cos_in, sin_in, present_in, keymask_in,
        share_in, pairs_in,
        ids_out, fin_out, ng_out, stats_out, ge_out,
        pool, W7, GW, EX, GNB, sids, H0B, QKV, ATT, PS, H1, MIX, DF, DG, DQB, DB,
        INV, YS, YR, PB, PROW, PM, XR, ZS, ZR, CRA, YRA, NGS, NGR, NGZ, SQ, SQS, FG, TABLE,
        ssem, rsem, lsem,
    ) = refs
    r = lax.axis_index("rep")
    f = lax.axis_index("fsdp")
    d = r * NF + f
    z, x = lax.div(f, NX), lax.rem(f, NX)
    g, t = lax.div(r, TP), lax.rem(r, TP)
    y, c = lax.div(t, 2), lax.rem(t, 2)
    ty = (1 - y) * 2 + c
    tc = y * 2 + 1 - c
    tyc = (1 - y) * 2 + 1 - c
    dev_x = (r, z * NX + 1 - x)
    dev_y = (g * TP + ty, f)
    dev_c = (g * TP + tc, f)

    GATE, UP, PT, PT2 = 0, 4 * S, 8 * S, 12 * S
    CR, CR2 = 16 * S, 18 * S
    H0F, H1F, HAT, DS2, DS1, DQ = 20 * S, 21 * S, 22 * S, 25 * S, 26 * S, 27 * S

    def blk(offset, index=0):
        return pl.ds(pl.multiple_of(offset + index * S, 128), S)

    sem_at = {}
    for name, many in (
        ("ids", 1), ("gn", 1), ("ex", NZ), ("ez", NZ), ("wu", 4 * NZ), ("wd", 4 * NZ), ("wx", 4 * NZ),
        ("ay", NF), ("ac", 2 * NF), ("h1", 3), ("fc", 2), ("fy", 1), ("pool", 1), ("df", 3),
        ("bc", 2), ("by", 1), ("gx", 4 * NZ), ("gz", 4 * NZ), ("qc", 2), ("qy", 1), ("nc", 1), ("ny", 1),
        ("nx", 1), ("nz", NZ), ("ng", NG), ("fin", 3), ("gg", NG), ("sq", 1), ("eu", 2 * NZ), ("ed", 2 * NZ),
        ("gex", NZ), ("gey", NZ), ("gez", 2 * NZ), ("e1", 1), ("e3", 4), ("eg", NG),
    ):
        sem_at[name] = (sum(n for _, n in sem_at.values()), many)
    later = []

    def copy(name, index, src, dst, dev, landing=None):
        base = sem_at[name][0]
        return pltpu.make_async_remote_copy(
            src_ref=src, dst_ref=dst, send_sem=ssem.at[base + index],
            recv_sem=rsem.at[base + (index if landing is None else landing)],
            device_id=dev, device_id_type=MESH,
        )

    def send(name, index, src, dst, dev, only=None, landing=None):
        def start():
            copy(name, index, src, dst, dev, landing).start()

        def finish():
            copy(name, index, src, dst, dev, landing).wait_send()

        if only is None:
            start()
            later.append(finish)
        else:
            pl.when(only)(start)
            later.append(lambda: pl.when(only)(finish))

    def arrive(name, index, dst, only=None):
        def wait():
            sem = rsem.at[sem_at[name][0] + index]
            pltpu.make_async_copy(dst, dst, sem).wait()

        if only is None:
            wait()
        else:
            pl.when(only)(wait)

    def spread(name, src, dst):
        base = sem_at[name][0]

        def one(k, carry):
            to = lax.rem(d + k, N)
            pltpu.make_async_remote_copy(
                src_ref=src, dst_ref=dst.at[d], send_sem=ssem.at[base], recv_sem=rsem.at[base],
                device_id=(lax.div(to, NF), lax.rem(to, NF)), device_id_type=MESH,
            ).start()
            return carry

        lax.fori_loop(1, N, one, 0)
        rest = dst.at[pl.ds(0, N - 1)]
        later.append(lambda: pltpu.make_async_copy(rest, rest, ssem.at[base]).wait())

    def gather_all(name, dst):
        rest = dst.at[pl.ds(0, N - 1)]
        pltpu.make_async_copy(rest, rest, rsem.at[sem_at[name][0]]).wait()

    def keep(only, ref, at, value):
        @pl.when(only)
        def _():
            ref[at] = value

    def load(src, dst, sem):
        done = pltpu.make_async_copy(src, dst, lsem.at[sem])
        done.start()
        return done

    table = TABLE if rows % 8 else pool.at[pl.ds(0, rows)]
    got_table = load(table_in, table, 0)
    slots = [t, 4, 5, 6]

    def wrow(index):
        return pl.ds(pl.multiple_of(index * nr, 16), nr)

    got_piece = [load(pieces_in.at[t, m], W7.at[slots[m], wrow(f)], 1 + m) for m in range(4)]
    got_ids = load(ids_in, ids_out.at[d], 5)
    got_gn = load(gn_in, GNB.at[f], 6)
    barrier = pltpu.get_barrier_semaphore()

    def greet(k, carry):
        to = lax.rem(d + k, N)
        pl.semaphore_signal(
            barrier, inc=1, device_id=(lax.div(to, NF), lax.rem(to, NF)), device_id_type=MESH
        )
        return carry

    lax.fori_loop(1, N, greet, 0)
    got_ids.wait()
    got_gn.wait()
    for item in got_piece:
        item.wait()
    pl.semaphore_wait(barrier, N - 1)

    spread("ids", ids_out.at[d], ids_out)
    base = sem_at["gn"][0]

    def gn_one(k, carry):
        pltpu.make_async_remote_copy(
            src_ref=GNB.at[f], dst_ref=GNB.at[f], send_sem=ssem.at[base], recv_sem=rsem.at[base],
            device_id=(r, lax.rem(f + k, NF)), device_id_type=MESH,
        ).start()
        return carry

    lax.fori_loop(1, NF, gn_one, 0)
    gn_rest = GNB.at[pl.ds(0, NF - 1)]
    later.append(lambda: pltpu.make_async_copy(gn_rest, gn_rest, ssem.at[base]).wait())

    def piece(m, origin_z, origin_x):
        return W7.at[slots[m], wrow(origin_z * NX + origin_x)]

    def up_to(m, origin, only):
        send("wu", m * NZ + origin, piece(m, origin, x), piece(m, origin, x), (r, f + NX), only)

    def down_to(m, origin, only):
        send("wd", m * NZ + origin, piece(m, origin, x), piece(m, origin, x), (r, f - NX), only)

    def across(m, origin, only=None):
        send("wx", m * NZ + origin, piece(m, origin, x), piece(m, origin, x), dev_x, only)

    def own_pieces(m):
        up_to(m, z, z + 1 < NZ)
        down_to(m, z, z >= 1)
        across(m, z)

    def relay(m):
        for k in range(1, NZ):
            low, high = z - k, z + k
            below, above = jnp.maximum(low, 0), jnp.minimum(high, NZ - 1)
            arrive("wu", m * NZ + below, piece(m, below, x), low >= 0)
            up_to(m, below, (low >= 0) & (z + 1 < NZ))
            across(m, below, low >= 0)
            arrive("wd", m * NZ + above, piece(m, above, x), high < NZ)
            down_to(m, above, (high < NZ) & (z >= 1))
            across(m, above, high < NZ)

    own_pieces(0)
    own_pieces(1)

    gather_all("ids", ids_out)
    got_sids = load(ids_out.at[pl.ds(pl.multiple_of(r * NF, NF), NF)], sids, 5)
    got_sids.wait()
    got_table.wait()
    start_row = f * rows
    EXS, EXO, EXR, EZR = (EX.at[i] for i in range(4))

    def rows_of(other, store):
        stage = pool.at[pl.ds(0 if rows % 8 else rows, S)]

        def block(i, carry):
            owner = i * NX + other

            def token(j, inner):
                wanted = sids[owner, 0, j] - start_row
                inside = (wanted >= 0) & (wanted < rows)
                row = table[pl.ds(jnp.clip(wanted, 0, rows - 1), 1), :]
                stage[pl.ds(j, 1), :] = jnp.where(inside, row, 0.0)
                return inner

            lax.fori_loop(0, S, token, 0, unroll=8)
            store(i, stage[...].astype(BF))
            return carry

        lax.fori_loop(0, NZ, block, 0)

    def store_other(i, value):
        EXS[i] = value

    def store_own(i, value):
        EXO[i] = value

    rows_of(1 - x, store_other)
    for i in range(NZ):
        send("ex", i, EXS.at[i], EXR.at[i], dev_x)
    rows_of(x, store_own)
    relay(0)
    own_pieces(2)
    for i in range(NZ):
        arrive("ex", i, EXR.at[i])
        total = EXO[i] + EXR[i]
        EXO[i] = total
        keep(z == i, EZR, i, total)
        send("ez", i, EXO.at[i], EZR.at[z], (r, i * NX + x), z != i, z)

    for i in range(NZ):
        arrive("wx", i, piece(0, i, 1 - x))
    for i in range(NF):
        here = W7.at[t, wrow(i)]
        send("ay", i, here, here, dev_y)
        send("ac", i, here, here, dev_c)
    relay(1)
    own_pieces(3)
    for i in range(NF):
        there = W7.at[ty, wrow(i)]
        arrive("ay", i, there)
        send("ac", NF + i, there, there, dev_c)

    arrive("gn", 0, gn_rest)
    tiles = jnp.concatenate([GNB[i] for i in range(NF)], axis=1).astype(BF)
    at_row = lax.broadcasted_iota(jnp.int32, (NF * 128, D), 0)
    at_col = lax.broadcasted_iota(jnp.int32, (NF * 128, D), 1)
    lane = lax.bitwise_and(at_row, 127)
    pick = (lane < nr) & (lax.shift_right_logical(at_row, 7) * nr + lane == at_col)
    gains = dot(tiles, jnp.where(pick, 1.0, 0.0).astype(BF))
    gain = [gains[i : i + 1] for i in range(6)]

    for i in range(NZ):
        pl.when(z != i)(functools.partial(arrive, "ez", i, EZR.at[i]))
    embedded = EZR[0].astype(F32)
    for i in range(1, NZ):
        embedded = embedded + EZR[i].astype(F32)
    normed, hat, inverse = layer_norm(embedded, gain[0], gain[1])
    pool[blk(H0F), :] = normed
    pool[blk(HAT, 0), :] = hat
    INV[0] = inverse
    H0B[...] = normed.astype(BF)
    relay(2)

    for i in range(NF):
        arrive("ac", i, W7.at[tc, wrow(i)])
    for i in range(NF):
        arrive("ac", NF + i, W7.at[tyc, wrow(i)])
    tables = [jnp.concatenate([ref[...]] * (D // 128), axis=1) for ref in (cos_in, sin_in)]
    in_half = lax.bitwise_and(lax.broadcasted_iota(jnp.int32, (S, D), 1), HD - 1) < HD // 2

    def turn(values, sign):
        partner = jnp.where(
            in_half, pltpu.roll(values, D - HD // 2, 1), pltpu.roll(values, HD // 2, 1)
        )
        signed = jnp.where(in_half, -sign, sign) * tables[1]
        return values * tables[0] + partner * signed

    for j in range(3):
        projected = dot(H0B[...], W7[j])
        QKV[j] = (turn(projected, 1.0) if j < 2 else projected).astype(BF)
    allowed = keymask_in[...][0:1, :] > 0.0
    scaling = HD ** (-0.5)
    first_half = lax.broadcasted_iota(jnp.int32, (S, 128), 1) < HD

    def half(values, which):
        keep = first_half if which == 0 else jnp.logical_not(first_half)
        return jnp.where(keep, values, jnp.zeros_like(values))

    def attend(p, carry):
        lanes = pl.ds(pl.multiple_of(p * 128, 128), 128)
        query, keys, values = QKV[0, :, lanes], QKV[1, :, lanes], QKV[2, :, lanes]
        result = jnp.zeros((S, 128), F32)
        for which in range(2):
            scores = dot_nt(query, half(keys, which)) * scaling
            scores = jnp.where(allowed, scores, -1000000000.0)
            raised = jnp.exp(scores - jnp.max(scores, axis=-1, keepdims=True))
            chances = raised / jnp.sum(raised, axis=-1, keepdims=True)
            PS[2 * p + which] = chances
            result = result + dot(chances.astype(BF), half(values, which))
        ATT[:, lanes] = result.astype(BF)
        return carry

    lax.fori_loop(0, D // 128, attend, 0)
    branch = dot(ATT[...], W7[3])
    normed, hat, inverse = layer_norm(pool[blk(H0F), :] + branch, gain[2], gain[3])
    pool[blk(H1F), :] = normed
    pool[blk(HAT, 1), :] = hat
    INV[1] = inverse
    H1[t] = normed.astype(BF)

    def share(name, buffer):
        send(name, 0, buffer.at[t], buffer.at[t], dev_y)
        send(name, 1, buffer.at[t], buffer.at[t], dev_c)
        arrive(name, 0, buffer.at[ty])
        send(name, 2, buffer.at[ty], buffer.at[ty], dev_c)
        arrive(name, 1, buffer.at[tc])
        arrive(name, 2, buffer.at[tyc])

    def reduce(names, offset, landing, which):
        for i in range(2):
            send(names[0], i, pool.at[blk(offset, i * 2 + 1 - c)], pool.at[blk(landing, i)], dev_c)
        for i in range(2):
            arrive(names[0], i, pool.at[blk(landing, i)])
        away = pool[blk(offset, (1 - y) * 2 + c), :] + pool[blk(landing, 1 - y), :]
        YS[which] = away.astype(BF)
        send(names[1], 0, YS.at[which], YR.at[which], dev_y)
        mine = pool[blk(offset, t), :] + pool[blk(landing, y), :]
        arrive(names[1], 0, YR.at[which])
        return mine + YR[which].astype(F32)

    share("h1", H1)
    relay(3)
    for m in range(1, 4):
        for i in range(NZ):
            arrive("wx", m * NZ + i, piece(m, i, 1 - x))

    def forward(b, carry):
        gate, up = dot(H1[b], W7[4]), dot(H1[b], W7[5])
        pool[blk(GATE, b), :] = gate
        pool[blk(UP, b), :] = up
        mixed = (gate / (1.0 + jnp.exp(-gate)) * up).astype(BF)
        MIX[b] = mixed
        pool[blk(PT, b), :] = dot(mixed, W7[6])
        return carry

    lax.fori_loop(0, TP, forward, 0)
    feed = reduce(("fc", "fy"), PT, CR, 0)
    normed, hat, inverse = layer_norm(pool[blk(H1F), :] + feed, gain[4], gain[5])
    pool[blk(HAT, 2), :] = hat
    INV[2] = inverse
    PROW[0] = jnp.sum(normed * present_in[...][:, 0:1], axis=0, keepdims=True) / share_in[...][0:1, 0:1]

    spread("pool", PROW.at[0], PB)
    PB[d] = PROW[0]
    gather_all("pool", PB)
    for i in range(N):
        PM[pl.ds(i, 1), :] = PB[i]
    pooled = PM[...]
    wide = lax.broadcasted_iota(jnp.int32, (N, D), 1)
    row_at = lax.broadcasted_iota(jnp.int32, (N, N), 0)
    col_at = lax.broadcasted_iota(jnp.int32, (N, N), 1)
    paired = pairs_in[...]
    loss_value = jnp.zeros((1, 1), F32)
    d_pooled = jnp.zeros((N, D), F32)
    for width in (D // 12, D // 3, D):
        portion = jnp.where(wide < width, pooled, 0.0)
        inverse = lax.rsqrt(jnp.sum(portion * portion, axis=1, keepdims=True) + 1e-06)
        unit = portion * inverse
        similar = lax.dot_general(
            unit, unit, (((1,), (1,)), ((), ())), precision=HI, preferred_element_type=F32
        ) / logit_divisor
        similar = jnp.where(row_at == col_at, -1000000000.0, similar)
        row_max = jnp.max(similar, axis=1, keepdims=True)
        raised = jnp.exp(similar - row_max)
        total = jnp.sum(raised, axis=1, keepdims=True)
        target = jnp.sum(jnp.where(paired > 0.0, similar, 0.0), axis=1, keepdims=True)
        term = row_max + jnp.log(total) - target
        loss_value = loss_value + jnp.sum(term, axis=0, keepdims=True) / N
        col_max = jnp.max(similar, axis=0, keepdims=True)
        raised_t = jnp.exp(similar - col_max)
        turned = raised_t / jnp.sum(raised_t, axis=0, keepdims=True)
        d_similar = (raised / total + turned - 2.0 * paired) / (3.0 * N) / logit_divisor
        d_unit = lax.dot_general(
            d_similar, unit, (((1,), (0,)), ((), ())), precision=HI, preferred_element_type=F32
        )
        inner = jnp.sum(d_unit * unit, axis=1, keepdims=True)
        d_pooled = d_pooled + inverse * (d_unit - unit * inner)
    loss_value = loss_value / 3.0
    own_row = lax.broadcasted_iota(jnp.int32, (N, D), 0) == d
    d_mine = jnp.sum(jnp.where(own_row, d_pooled, 0.0), axis=0, keepdims=True)

    d_two = d_mine * present_in[...][:, 0:1] / share_in[...][0:1, 0:1]
    d_sum, d_gain_two, d_shift_two = norm_back(d_two, pool[blk(HAT, 2), :], INV[2], gain[4])
    pool[blk(DS2), :] = d_sum
    DF[t] = d_sum.astype(BF)
    share("df", DF)

    def back(b, carry):
        d_mixed = dot_nt(DF[b], W7[6])
        gate, up = pool[blk(GATE, b), :], pool[blk(UP, b), :]
        logistic = 1.0 / (1.0 + jnp.exp(-gate))
        d_gate = (d_mixed * up * (logistic * (1.0 + gate * (1.0 - logistic)))).astype(BF)
        d_up = (d_mixed * (gate * logistic)).astype(BF)
        DG[0, b] = d_gate
        DG[1, b] = d_up
        pool[blk(PT2, b), :] = dot_nt(d_gate, W7[4]) + dot_nt(d_up, W7[5])
        return carry

    TILE = 256

    def product(left, right, m):
        def tile(i, carry):
            at = pl.ds(pl.multiple_of(i * TILE, TILE), TILE)
            GW[m, at, :] = dot_tn(left(at), right()).astype(BF)
            return carry

        lax.fori_loop(0, D // TILE, tile, 0)

    def part(m, i, other):
        return GW.at[slots[m], wrow(i * NX + other)]

    def give(m):
        for i in range(NZ):
            send("gx", m * NZ + i, part(m, i, 1 - x), XR.at[m, i], dev_x)

    def pass_on(m):
        for i in range(NZ):
            arrive("gx", m * NZ + i, XR.at[m, i])
            total = (part(m, i, x)[...].astype(F32) + XR[m, i].astype(F32)).astype(BF)
            ZS[m, i] = total
            keep(z == i, ZR, (m, i), total)
            send("gz", m * NZ + i, ZS.at[m, i], ZR.at[m, z], (r, i * NX + x), z != i, m * NZ + z)

    def product_rows(buffer):
        return lambda at: buffer[:, :, at].reshape(TP * S, TILE)

    product(product_rows(MIX), lambda: DF[...].reshape(TP * S, D), 6)
    give(3)
    lax.fori_loop(0, TP, back, 0)
    for i in range(2):
        send("bc", i, pool.at[blk(PT2, i * 2 + 1 - c)], pool.at[blk(CR2, i)], dev_c)
    product(product_rows(H1), lambda: DG[0].reshape(TP * S, D), 4)
    give(1)
    for i in range(2):
        arrive("bc", i, pool.at[blk(CR2, i)])
    away = pool[blk(PT2, (1 - y) * 2 + c), :] + pool[blk(CR2, 1 - y), :]
    YS[1] = away.astype(BF)
    send("by", 0, YS.at[1], YR.at[1], dev_y)
    product(product_rows(H1), lambda: DG[1].reshape(TP * S, D), 5)
    give(2)
    pass_on(3)
    mine = pool[blk(PT2, t), :] + pool[blk(CR2, y), :]
    arrive("by", 0, YR.at[1])
    d_one = pool[blk(DS2), :] + (mine + YR[1].astype(F32))

    d_sum, d_gain_one, d_shift_one = norm_back(d_one, pool[blk(HAT, 1), :], INV[1], gain[2])
    pool[blk(DS1), :] = d_sum
    DB[0] = d_sum.astype(BF)
    product(lambda at: ATT[:, at], lambda: DB[0], 3)
    DB[1] = dot_nt(DB[0], W7[3]).astype(BF)
    pass_on(1)

    def attend_back(p, carry):
        lanes = pl.ds(pl.multiple_of(p * 128, 128), 128)
        query, keys, values = QKV[0, :, lanes], QKV[1, :, lanes], QKV[2, :, lanes]
        grad = DB[1, :, lanes]
        d_query = jnp.zeros((S, 128), F32)
        d_keys = jnp.zeros((S, 128), F32)
        d_values = jnp.zeros((S, 128), F32)
        for which in range(2):
            chances = PS[2 * p + which]
            d_values = d_values + dot_tn(chances.astype(BF), half(grad, which))
            d_chances = dot_nt(grad, half(values, which))
            inner = jnp.sum(chances * d_chances, axis=-1, keepdims=True)
            d_scores = (chances * (d_chances - inner)).astype(BF)
            d_query = d_query + dot(d_scores, half(keys, which)) * scaling
            d_keys = d_keys + dot_tn(d_scores, half(query, which)) * scaling
        pool[blk(DQ, 0), lanes] = d_query
        pool[blk(DQ, 1), lanes] = d_keys
        DQB[2, :, lanes] = d_values.astype(BF)
        return carry

    lax.fori_loop(0, D // 128, attend_back, 0)
    for j in range(2):
        DQB[j] = turn(pool[blk(DQ, j), :], -1.0).astype(BF)

    def attend_weights(j, carry):
        def tile(i, inner):
            at = pl.ds(pl.multiple_of(i * TILE, TILE), TILE)
            GW[j, at, :] = dot_tn(H0B[:, at], DQB[j]).astype(BF)
            return inner

        return lax.fori_loop(0, D // TILE, tile, carry)

    lax.fori_loop(0, 3, attend_weights, 0)
    for i in range(2):
        send("qc", i, GW.at[i * 2 + 1 - c], CRA.at[i], dev_c)
    d_zero = pool[blk(DS1), :]
    for j in range(3):
        d_zero = d_zero + dot_nt(DQB[j], W7[j])
    d_embedded, d_gain_zero, d_shift_zero = norm_back(d_zero, pool[blk(HAT, 0), :], INV[0], gain[0])
    DB[2] = d_embedded.astype(BF)

    got_own = load(DB.at[2], ge_out.at[d], 0)
    cols = [pl.ds(0, D // 2), pl.ds(D // 2, D // 2)]

    def ge(order, origin):
        return ge_out.at[r * NF + origin * NX + x, :, cols[order]]

    def ge_up(order, origin, src, only):
        send("eu", order * NZ + origin, src, ge(order, origin), (r, f + NX), only)

    def ge_down(order, origin, src, only):
        send("ed", order * NZ + origin, src, ge(order, origin), (r, f - NX), only)

    for order in range(2):
        ge_up(order, z, DB.at[2, :, cols[order]], z + 1 < NZ)
        ge_down(order, z, DB.at[2, :, cols[order]], z >= 1)

    NGS[0] = jnp.concatenate(
        [d_gain_zero, d_shift_zero, d_gain_one, d_shift_one, d_gain_two, d_shift_two,
         jnp.zeros((2, D), F32)], axis=0)
    stages = (("nc", dev_c), ("ny", dev_y), ("nx", dev_x))
    for i, (name, dev) in enumerate(stages):
        send(name, 0, NGS.at[i], NGR.at[i], dev)
        arrive(name, 0, NGR.at[i])
        NGS[i + 1] = NGS[i] + NGR[i]
    for i in range(NZ):
        send("nz", i, NGS.at[3], NGZ.at[z], (r, i * NX + x), z != i, z)
        keep(z == i, NGZ, i, NGS[3])

    pass_on(2)
    for i in range(2):
        arrive("qc", i, CRA.at[i])

    def add_mats(target, other):
        def tile(i, carry):
            at = pl.ds(pl.multiple_of(i * TILE, TILE), TILE)
            GW[target, at, :] = (GW[target, at, :].astype(F32) + other[at, :].astype(F32)).astype(BF)
            return carry

        lax.fori_loop(0, D // TILE, tile, 0)

    add_mats(ty, CRA.at[1 - y])
    send("qy", 0, GW.at[ty], YRA, dev_y)
    add_mats(t, CRA.at[y])
    got_own.wait()

    for k in range(1, NZ):
        low, high = z - k, z + k
        below, above = jnp.maximum(low, 0), jnp.minimum(high, NZ - 1)
        for order in range(2):
            arrive("eu", order * NZ + below, ge(order, below), low >= 0)
            ge_up(order, below, ge(order, below), (low >= 0) & (z + 1 < NZ))
            arrive("ed", order * NZ + above, ge(order, above), high < NZ)
            ge_down(order, above, ge(order, above), (high < NZ) & (z >= 1))

    def line(rep, which_x, order, i):
        return ge_out.at[rep * NF + i * NX + which_x, :, cols[order]]

    def all_of(rep, order):
        return ge_out.at[pl.ds(pl.multiple_of(rep * NF, NF), NF), :, cols[order]]

    ry, rc, ryc = g * TP + ty, g * TP + tc, g * TP + tyc
    for i in range(NZ):
        copy_at = line(r, x, 0, i)
        send("gex", i, copy_at, copy_at, dev_x)
    for i in range(NZ):
        copy_at = line(r, x, 1, i)
        send("gey", i, copy_at, copy_at, dev_y)

    arrive("qy", 0, YRA)
    add_mats(t, YRA)
    give(0)

    for i in range(NZ):
        arrive("gex", i, line(r, 1 - x, 0, i))
    send("e1", 0, all_of(r, 0), all_of(r, 0), dev_y)
    send("e3", 0, all_of(r, 0), all_of(r, 0), dev_c)
    for i in range(NZ):
        arrive("gey", i, line(ry, x, 1, i))
    for i in range(NZ):
        for which, rep in enumerate((r, ry)):
            copy_at = line(rep, x, 1, i)
            send("gez", which * NZ + i, copy_at, copy_at, dev_x)
    pass_on(0)

    for i in range(NZ):
        pl.when(z != i)(functools.partial(arrive, "nz", i, NGZ.at[i]))
    total_norms = NGZ[0]
    for i in range(1, NZ):
        total_norms = total_norms + NGZ[i]

    for m in (3, 1, 2, 0):
        for i in range(NZ):
            pl.when(z != i)(functools.partial(arrive, "gz", m * NZ + i, ZR.at[m, i]))
        total = ZR[m, 0].astype(F32)
        for i in range(1, NZ):
            total = total + ZR[m, i].astype(F32)
        fin_out[t, pl.ds(m * nr, nr), :] = total.astype(BF)

    if NG > 1:
        FG[g] = fin_out[t]
        for k in range(1, NG):
            other = lax.rem(g + k, NG)
            send("gg", k, FG.at[g], FG.at[g], (other * TP + t, f), None, g)
        for k in range(1, NG):
            other = lax.rem(g + k, NG)
            arrive("gg", other, FG.at[other])
        total = FG[0].astype(F32)
        for k in range(1, NG):
            total = total + FG[k].astype(F32)
        fin_out[t] = total.astype(BF)
    own = fin_out[t].astype(F32)
    squares = jnp.where(g == 0, jnp.sum(own * own), 0.0)
    share("fin", fin_out)

    arrive("e1", 0, all_of(ry, 0))
    send("e3", 1, all_of(ry, 0), all_of(ry, 0), dev_c)
    for i in range(NZ):
        for which, rep in enumerate((r, ry)):
            arrive("gez", which * NZ + i, line(rep, 1 - x, 1, i))
    send("e3", 2, all_of(r, 1), all_of(r, 1), dev_c)
    send("e3", 3, all_of(ry, 1), all_of(ry, 1), dev_c)
    for which, (rep, order) in enumerate(((rc, 0), (ryc, 0), (rc, 1), (ryc, 1))):
        arrive("e3", which, all_of(rep, order))
    if NG > 1:

        def group(which):
            return ge_out.at[pl.ds(pl.multiple_of(which * TP * NF, TP * NF), TP * NF)]

        for k in range(1, NG):
            other = lax.rem(g + k, NG)
            send("eg", k, group(g), group(g), (other * TP + t, f), None, g)
        for k in range(1, NG):
            other = lax.rem(g + k, NG)
            arrive("eg", other, group(other))

    def fetch(b):
        return pltpu.make_async_copy(
            ge_out.at[pl.ds(b * NZ, NZ)], EX.at[2 + lax.rem(b, 2)], lsem.at[1 + lax.rem(b, 2)]
        )

    fetch(0).start()

    def pairs_of(b, carry):
        pl.when(b + 1 < N // NZ)(lambda: fetch(b + 1).start())
        fetch(b).wait()
        for i in range(NZ):
            both = dot_nt(DB[2], EX[2 + lax.rem(b, 2), i])
            carry = carry + jnp.where(idcol_in[...] == ids_out[b * NZ + i], both, 0.0)
        return carry

    both = lax.fori_loop(0, N // NZ, pairs_of, jnp.zeros((S, S), F32))
    squares = squares + jnp.sum(both)
    squares = squares + jnp.where(d == 0, jnp.sum(total_norms * total_norms), 0.0)
    SQ[0] = jnp.zeros((1, 128), F32) + squares
    spread("sq", SQ.at[0], SQS)
    SQS[d] = SQ[0]
    ng_out[...] = total_norms
    gather_all("sq", SQS)
    all_squares = SQS[0]
    for i in range(1, N):
        all_squares = all_squares + SQS[i]
    stats_out[...] = jnp.concatenate(
        [jnp.zeros((1, 128), F32) + loss_value, jnp.sqrt(all_squares), jnp.zeros((6, 128), F32)], axis=0
    )
    arrive_last = later
    for finish in arrive_last:
        finish()


def run_step(sizes, *args):
    NR, NF, S, D, rows = sizes
    NZ, NG = NF // 2, NR // TP
    N, nr = NR * NF, D // NF
    vmem = pl.BlockSpec(memory_space=pltpu.VMEM)
    hbm = pl.BlockSpec(memory_space=pl.ANY)
    sems = 13 + 23 * NZ + 3 * NF + 3 * NG + 27 + 8 * NZ
    shapes = [
        ((30 * S if rows % 8 else max(rows + S, 30 * S), D), F32),
        ((7, D, D), BF), ((7, D, D), BF), ((4, NZ, S, D), BF), ((NF, 8, 128), F32), None,
        ((S, D), BF), ((3, S, D), BF), ((S, D), BF), ((D // HD, S, S), F32), ((TP, S, D), BF),
        ((TP, S, D), BF), ((TP, S, D), BF), ((2, TP, S, D), BF), ((3, S, D), BF), ((3, S, D), BF),
        ((3, S, 1), F32), ((2, S, D), BF), ((2, S, D), BF), ((N, 1, D), F32), ((1, 1, D), F32), ((N, D), F32),
        ((4, NZ, nr, D), BF), ((4, NZ, nr, D), BF), ((4, NZ, nr, D), BF), ((2, D, D), BF), ((D, D), BF),
        ((4, 8, D), F32), ((3, 8, D), F32), ((NZ, 8, D), F32), ((1, 1, 128), F32), ((N, 1, 128), F32),
        ((NG, 4 * nr, D) if NG > 1 else (1, 16, 128), BF), ((rows, D) if rows % 8 else (8, 128), F32),
    ]
    scratch = [pltpu.VMEM(*item) if item else pltpu.SMEM((NF, 1, S), jnp.int32) for item in shapes]
    return pl.pallas_call(
        functools.partial(step_kernel, sizes),
        name="step",
        out_shape=(
            jax.ShapeDtypeStruct((N, 1, S), jnp.int32),
            jax.ShapeDtypeStruct((TP, 4 * nr, D), BF),
            jax.ShapeDtypeStruct((8, D), F32),
            jax.ShapeDtypeStruct((8, 128), F32),
            jax.ShapeDtypeStruct((N, S, D), BF),
        ),
        in_specs=[vmem, vmem, vmem, hbm, hbm] + [vmem] * 6,
        out_specs=(vmem, vmem, vmem, vmem, hbm),
        scratch_shapes=scratch
        + [pltpu.SemaphoreType.DMA((sems,)), pltpu.SemaphoreType.DMA((sems,)), pltpu.SemaphoreType.DMA((8,))],
        compiler_params=pltpu.CompilerParams(
            collective_id=0, has_side_effects=True, vmem_limit_bytes=67_000_000
        ),
    )(*args)


def adamw(weight, grad, first, second, rate):
    first_new = beta_first * first + (1.0 - beta_first) * grad
    second_new = beta_second * second + (1.0 - beta_second) * grad * grad
    first_fix = 1.0 - beta_first**STEP
    second_fix = 1.0 - beta_second**STEP
    update = first_new / first_fix / (jnp.sqrt(second_new / second_fix) + adam_floor)
    return (weight - rate * (update + weight_decay * weight), first_new, second_new)


def table_kernel(sizes, ids, ge, factor, w, m, v, w_out, m_out, v_out, grads, landing, stage, sems):
    NR, NF, S, D, rows = sizes
    N = NR * NF
    step = pl.program_id(0)
    block = w.shape[0]

    @pl.when(step == 0)
    def _():
        start_row = lax.axis_index("fsdp") * rows

        def fetch(s):
            return pltpu.make_async_copy(ge.at[s], landing.at[lax.rem(s, 4)], sems.at[lax.rem(s, 4)])

        for s in range(3):
            fetch(s).start()

        def clear(i, carry):
            grads[pl.ds(pl.multiple_of(i * block, 8), block), :] = jnp.zeros((block, D), F32)
            return carry

        lax.fori_loop(0, grads.shape[0] // block, clear, 0)

        def sequence(s, carry):
            pl.when(s + 3 < N)(lambda: fetch(s + 3).start())
            fetch(s).wait()
            stage[...] = landing[lax.rem(s, 4)].astype(F32)

            def token(j, inner):
                wanted = ids[s, 0, j] - start_row

                @pl.when((wanted >= 0) & (wanted < rows))
                def _():
                    at = pl.ds(wanted, 1)
                    grads[at, :] = grads[at, :] + stage[pl.ds(j, 1), :]

                return inner

            return lax.fori_loop(0, S, token, carry)

        lax.fori_loop(0, N, sequence, 0)

    grad = grads[pl.ds(pl.multiple_of(step * block, 8), block), :] * factor[0:1, 0:1]
    w_out[...], m_out[...], v_out[...] = adamw(w[...], grad, m[...], v[...], learn_rate)


def update_table(sizes, ids, ge, factor, w, m, v):
    NR, NF, S, D, rows = sizes
    block = 424
    steps = pl.cdiv(rows, block)
    part = pl.BlockSpec((block, D), lambda i: (i, 0))
    return pl.pallas_call(
        functools.partial(table_kernel, sizes),
        name="table",
        grid=(steps,),
        out_shape=(jax.ShapeDtypeStruct((rows, D), F32),) * 3,
        in_specs=[
            pl.BlockSpec(memory_space=pltpu.SMEM), pl.BlockSpec(memory_space=pl.ANY),
            pl.BlockSpec((8, 128), lambda i: (0, 0)), part, part, part,
        ],
        out_specs=(part, part, part),
        scratch_shapes=[
            pltpu.VMEM((steps * block, D), F32), pltpu.VMEM((4, S, D), BF), pltpu.VMEM((S, D), F32),
            pltpu.SemaphoreType.DMA((4,)),
        ],
        compiler_params=pltpu.CompilerParams(vmem_limit_bytes=60_000_000),
    )(ids, ge, factor, w, m, v)


def local(
    sizes,
    token_ids,
    lengths,
    slot_order,
    pair_labels,
    embedding,
    attend_weight,
    attention_output_matrix,
    gate_up,
    contract_kernel,
    norm_params,
    embedding_first,
    embedding_second,
    attend_first,
    attend_second,
    output_first,
    output_second,
    gate_up_first,
    gate_up_second,
    down_first,
    down_second,
    norm_first,
    norm_second,
):
    NR, NF, S, D, rows = sizes
    nr = D // NF
    f = lax.axis_index("fsdp")
    length = lengths[0]
    positions = jnp.arange(S)
    present = (positions < length).astype(F32)
    angles = (
        positions.astype(F32)[:, None]
        * (1000.0 ** (-2.0 * jnp.arange(HD // 2).astype(F32) / HD))[None, :]
    )
    cosine, sine = jnp.tile(jnp.cos(angles), (1, 128 * 2 // HD)), jnp.tile(jnp.sin(angles), (1, 128 * 2 // HD))
    partner = pair_labels[slot_order]
    paired = (partner[:, None] == slot_order[None, :]).astype(F32)
    gains = jnp.zeros((8, 128), F32).at[:6, :nr].set(norm_params.astype(BF).astype(F32))
    attention = jnp.concatenate(
        [attend_weight.reshape(nr, 3, D).transpose(1, 0, 2), attention_output_matrix[None]], axis=0
    ).astype(BF)
    hidden = gate_up.astype(BF).reshape(nr, 2, NF, TP, nr).transpose(3, 1, 0, 2, 4).reshape(TP, 2, nr, D)
    down = contract_kernel.astype(BF).reshape(TP, 1, nr, D)
    pieces = jnp.concatenate([attention[:, None], hidden, down], axis=1)
    ids, fin, norms, stats, ge = run_step(
        sizes,
        token_ids.reshape(1, S),
        jnp.broadcast_to(token_ids.reshape(S, 1), (S, 128)),
        gains,
        embedding,
        pieces,
        cosine,
        sine,
        jnp.broadcast_to(present[:, None], (S, 128)),
        jnp.broadcast_to(present[None, :], (8, S)),
        jnp.broadcast_to(length.astype(F32), (8, 128)),
        paired,
    )
    loss_value, grad_norm = stats[0, 0], stats[1, 0]
    factor = jnp.minimum(1.0, clip_level / (grad_norm + 1e-06))
    emb_next = update_table(
        sizes, ids, ge, jnp.broadcast_to(factor, (8, 128)), embedding, embedding_first, embedding_second
    )
    fin = fin.reshape(TP, 4, nr, D)
    grad_attend = fin[:3, 0].transpose(1, 0, 2).reshape(nr, 3 * D).astype(F32)
    grad_output = fin[3, 0].astype(F32)
    grad_hidden = (
        fin[:, 1:3].reshape(TP, 2, nr, NF, nr).transpose(2, 1, 3, 0, 4).reshape(nr, 8 * D).astype(F32)
    )
    grad_down = fin[:, 3].reshape(TP * nr, D).astype(F32)
    grad_norms = lax.dynamic_slice(norms, (0, f * nr), (6, nr))
    att_next = adamw(attend_weight, grad_attend * factor, attend_first, attend_second, learn_rate)
    out_next = adamw(
        attention_output_matrix, grad_output * factor, output_first, output_second, learn_rate
    )
    gate_next = adamw(gate_up, grad_hidden * factor, gate_up_first, gate_up_second, learn_rate)
    down_next = adamw(contract_kernel, grad_down * factor, down_first, down_second, learn_rate)
    norm_next = adamw(norm_params, grad_norms * factor, norm_first, norm_second, norm_rate)
    return (
        loss_value, grad_norm, *emb_next, *att_next, *out_next, *gate_next, *down_next, *norm_next
    )


def solution(mesh):
    NR, NF = mesh.shape["rep"], mesh.shape["fsdp"]
    rows_spec, cols_spec = P("fsdp", None), P(None, "fsdp")

    def step(*args):
        S, D, rows = args[0].shape[1], args[4].shape[1], args[4].shape[0] // NF
        run = jax.shard_map(
            functools.partial(local, (NR, NF, S, D, rows)),
            mesh=mesh,
            in_specs=(P(("rep", "fsdp"), None), P(("rep", "fsdp")), P(), P())
            + (rows_spec,) * 5 + (cols_spec,) + (rows_spec,) * 10 + (cols_spec,) * 2,
            out_specs=(P(), P()) + (rows_spec,) * 15 + (cols_spec,) * 3,
            check_vma=False,
        )
        return run(*args)

    return step
```

time: 1750 us -> 424 us (0.24)
  waiting for transfers between devices: 1380 us -> 0 us
  Pallas kernels: 0 us -> 368 us
  blocking collectives: 142 us -> 0 us
  other arithmetic: 104 us -> 28.2 us
  matrix products: 61.4 us -> 0 us
  between operations: 25.2 us -> 2.26 us
    reduce_scatter x5 -> x0, waiting for transfers between devices: 693 us -> none  [the longest x1 316 us: local(): lax.psum_scatter(grad_gateup, 'fsdp', scatter_dimension=0, tiled=True)]
    pallas_call x0 -> x2, Pallas kernels: none -> 368 us  [the longest x1 263 us: run_step(): pl.pallas_call(functools.partial(step_kernel, sizes), name='step', out_sh...]
    all_gather x5 -> x0, waiting for transfers between devices: 343 us -> none  [the longest x1 138 us: local(): lax.all_gather(members[2], 'fsdp', axis=0, tiled=True)]
    psum x1 -> x0, waiting for transfers between devices: 281 us -> none  [local(): lax.psum((grad_table, shard_grads[0], shard_grads[1], shard_grads[2], sha...]
    all_gather x3 -> x0, blocking collectives: 114 us -> none  [the longest x1 65.8 us: local(): lax.all_gather(pooled[None, :], ('rep', 'fsdp'), axis=0, tiled=True)]
    unnamed x13 -> x0, waiting for transfers between devices: 62.6 us -> none
    dot_general x42 -> x0, matrix products: 61.4 us -> none  [the longest x1 7.96 us: local(): jnp.einsum('ld,lf->df', one_low, d_gateall, preferred_element_type=jnp.fl...]
    sub x6 -> x5, other arithmetic: 49 us -> 16.3 us  [adamw(): weight - rate * (update + weight_decay * weight)]
  transfers between devices with their start and end apart: 12 -> 0, of which waited for: 12 -> 0; matrix products, arithmetic and copies ran while one was open for 4% -> 0% of each run, Pallas kernels for 0% -> 0%
where the time goes in v1:
time: 424 us; the launch traced here: 423 us
  Pallas kernels  368 us (87%)
  other arithmetic  28.2 us (7%)
  local copies, waits for them, and re-layouts  24.4 us (6%)
    pallas_call x1, Pallas kernels, run_step(): pl.pallas_call(functools.partial(step_kernel, sizes), name='step', out_sh...  263 us
    pallas_call x1, Pallas kernels, update_table(): pl.pallas_call(functools.partial(table_kernel, sizes), name='table', grid...  105 us
    sub x5, other arithmetic, adamw(): weight - rate * (update + weight_decay * weight)  16.3 us
    mul x3, local copies, waits for them, and re-layouts, local(): grad_hidden * factor  12.1 us

profile of v1, /device:TPU:0, one launch (start us, length us, event | category | flops | bytes accessed | tf_op | source)
XLA Modules:
  0.0 422.9 jit_solution(779570479465441668)
XLA Ops:
  0.7 1.4 broadcast_in_dim.15.refs_1_
  2.0 0.7 convert_element_type.73
  2.7 0.6 pad_convert_fusion.refs_2_
  3.3 2.1 convert_element_type.75
  5.5 1.8 convert_element_type.74
  7.3 1.6 reshape.224
  9.1 1.3 reshape.225
  10.5 1.3 convert.12
  11.8 1.6 pad_maximum_fusion.refs_4_
  13.6 0.7 copy.46.refs_5_
  14.4 0.7 copy.47.refs_6_
  15.8 0.7 broadcast_in_dim.16.refs_7_
  16.5 0.6 broadcast_in_dim.17.refs_8_
  17.1 0.6 broadcast_in_dim.18.refs_9_
  17.7 0.7 gather_fusion
  18.4 0.7 compare_convert_fusion.refs_10_
  19.1 262.9 %step.1 = (s32[32,1,128]{2,1,0:T(1,128)}, bf16[4,384,768]{2,1,0:T(8,128)(2,1)}, f32[8,768]{1,0:T(8,128)}, f32[8,128]{1,0:T(8,128)}, bf16[32,128,768]{2,1,0:T(8,128)(2,1)}) custom-call(s32[1,128]{1,0:T(1,128)} %refs_0_.1, s32[128,128]{1,0:T(8,128)} %broadcast_in_dim.15.refs_1_, f32[8,128]{1,0:T(8,128)} %pad_convert_fusion.refs_2_, f32[3816,768]{1,0:T(8,128)} %w.1, ...), custom_call_target="tpu_custom_call" | custom-call | tf_op jit(solution)/shard_map/step/pallas_call | solution.py:743
  282.0 1.3 fusion.12
  284.0 0.6 broadcast_in_dim.20.factor
  284.6 105.1 %table.1 = (f32[3816,768]{1,0:T(8,128)}, f32[3816,768]{1,0:T(8,128)}, f32[3816,768]{1,0:T(8,128)}) custom-call(s32[32,1,128]{2,1,0:T(1,128)} %get-tuple-element.41.ids, bf16[32,128,768]{2,1,0:T(8,128)(2,1)} %get-tuple-element.42.ge, f32[8,128]{1,0:T(8,128)} %broadcast_in_dim.20.factor, f32[3816,768]{1,0:T(8,128)} %w.1, f32[3816,768]{1,0:T(8,128)} %m.1, ...), custom_call_target="tpu_custom_call" | custom-call | tf_op jit(solution)/shard_map/table/pallas_call | solution.py:822
  389.8 1.0 copy-done.4
  391.1 0.3 copy-done.12
  391.3 2.3 multiply_subtract_fusion.2
  393.7 1.2 multiply_subtract_fusion.3
  394.8 1.6 convert_multiply_fusion
  396.5 3.1 mul.274
  399.6 3.7 copy.55
  403.3 5.3 %mul.276 = f32[96,6144]{1,0:T(8,128)} reshape(f32[96,2,8,4,96]{4,3,2,1,0:T(4,128)} %bitcast.53) | data formatting | bytes 4718592 | tf_op jit(solution)/shard_map/mul | solution.py:916
  408.6 8.5 %multiply_subtract_fusion = (f32[96,6144]{1,0:T(8,128)}, f32[96,6144]{1,0:T(8,128)}, f32[96,6144]{1,0:T(8,128)}) fusion(f32[96,6144]{1,0:T(8,128)S(1)} %copy-done.2, f32[96,6144]{1,0:T(8,128)} %param.40, f32[96,6144]{1,0:T(8,128)} %mul.276, f32[96,6144]{1,0:T(8,128)} %param.41), kind=kLoop, calls=%fused_computation.5 | loop fusion | flops 8257536 | bytes 16515072 | tf_op jit(solution)/shard_map/sub | solution.py:769
  417.1 1.2 convert_multiply_fusion.1
  418.5 2.9 multiply_subtract_fusion.1
  421.5 1.4 multiply_subtract_fusion.4
  (49 shorter events, 1.1 us)
Async XLA Ops:
  0.7 17.0 %copy-start = (s32[32]{0:T(128)S(1)}, s32[32]{0:T(128)}, u32[]{:S(2)}) copy-start(s32[32]{0:T(128)} %param.27) | copy-start | bytes 388
  8.9 1.6 copy-start.7
  10.4 1.4 copy-start.5
  11.8 5.9 %copy-start.18 = (s32[32]{0:T(128)S(1)}, s32[32]{0:T(128)}, u32[]{:S(2)}) copy-start(s32[32]{0:T(128)} %param.26) | copy-start | bytes 388
  284.6 105.1 %copy-start.6 = (bf16[4,384,768]{2,1,0:T(8,128)(2,1)S(1)}, bf16[4,384,768]{2,1,0:T(8,128)(2,1)}, u32[]{:S(2)}) copy-start(bf16[4,384,768]{2,1,0:T(8,128)(2,1)} %get-tuple-element.46) | copy-start | bytes 7077892
  389.6 1.2 copy-start.4
  389.6 1.4 copy-start.11
  389.7 1.7 copy-start.12
  391.3 2.3 copy-start.8
  391.3 2.3 copy-start.13
  391.3 2.3 copy-start.14
  403.3 5.3 %copy-start.2 = (f32[96,6144]{1,0:T(8,128)S(1)}, f32[96,6144]{1,0:T(8,128)}, u32[]{:S(2)}) copy-start(f32[96,6144]{1,0:T(8,128)} %param.31) | copy-start | bytes 7077892
  408.6 9.8 %copy-start.9 = (f32[384,768]{1,0:T(8,128)S(1)}, f32[384,768]{1,0:T(8,128)}, u32[]{:S(2)}) copy-start(f32[384,768]{1,0:T(8,128)} %param.42) | copy-start | bytes 3538948
  408.6 9.8 %copy-start.10 = (f32[384,768]{1,0:T(8,128)S(1)}, f32[384,768]{1,0:T(8,128)}, u32[]{:S(2)}) copy-start(f32[384,768]{1,0:T(8,128)} %param.43) | copy-start | bytes 3538948
  417.1 1.4 copy-start.3
  417.1 5.8 %copy-start.1 = (s32[32]{0:T(128)S(1)}, s32[32]{0:T(128)}, u32[]{:S(2)}) copy-start(s32[32]{0:T(128)} %param.27) | copy-start | bytes 388
  418.5 2.9 copy-start.15
  418.5 2.9 copy-start.16
  418.5 2.9 copy-start.17

commit v2 on v1

v2 whole, which is shorter than its diff:
```python
import functools
import types

import jax
import jax.numpy as jnp
from jax import lax
from jax.experimental import pallas as pl
from jax.experimental.pallas import tpu as pltpu
from jax.sharding import PartitionSpec as P

H = 12
HD = 64
STEP = 4
TP = 4
MESH = pl.DeviceIdType.MESH
BF = jnp.bfloat16
F32 = jnp.float32

logit_divisor = 0.05
clip_level = 0.001
learn_rate = 0.02
norm_rate = 0.3
weight_decay = 0.01
beta_first = 0.5
beta_second = 0.75
adam_floor = 1e-08


def dot(a, b):
    return lax.dot_general(a, b, (((1,), (0,)), ((), ())), preferred_element_type=F32)


def dot_nt(a, b):
    return lax.dot_general(a, b, (((1,), (1,)), ((), ())), preferred_element_type=F32)


def dot_tn(a, b):
    return lax.dot_general(a, b, (((0,), (0,)), ((), ())), preferred_element_type=F32)


def layer_norm(values, gain, shift):
    centred = values - jnp.mean(values, axis=-1, keepdims=True)
    inverse = lax.rsqrt(jnp.mean(centred * centred, axis=-1, keepdims=True) + 1e-06)
    normed = centred * inverse
    return normed * gain + shift, normed, inverse


def norm_back(upstream, normed, inverse, gain):
    scaled = upstream * gain
    inner = (
        scaled
        - jnp.mean(scaled, axis=-1, keepdims=True)
        - normed * jnp.mean(scaled * normed, axis=-1, keepdims=True)
    )
    return (
        inner * inverse,
        jnp.sum(upstream * normed, axis=0, keepdims=True),
        jnp.sum(upstream, axis=0, keepdims=True),
    )


def step_layout(sizes):
    NR, NF, S, D, rows = sizes
    NZ, NG = NF // 2, NR // TP
    N, nr = NR * NF, D // NF
    block = (S, D)
    buffers = dict(
        pool=((max(0 if rows % 8 else rows, 30 * S), D), F32),
        table=((rows, D) if rows % 8 else (8, 128), F32),
        stage=(block, F32),
        W7=((7, D, D), BF),
        GW=((4, D, D), BF),
        EX=((4, NZ, S, D), BF),
        GNB=((NF, 8, 128), F32),
        H0B=(block, BF), QKV=((3, S, D), BF), ATT=(block, BF), PS=((D // HD, S, S), F32),
        H1=((TP, S, D), BF), MIX=((TP, S, D), BF), DF=((TP, S, D), BF), DG=((2, TP, S, D), BF),
        LX=((TP, S, D), BF), RX=((TP, S, D), BF), DQB=((3, S, D), BF), DB=((3, S, D), BF),
        INV=((3, S, 1), F32), YS=((2, S, D), BF), YR=((2, S, D), BF),
        PB=((N, 1, D), F32), PROW=((1, 1, D), F32), PM=((N, D), F32),
        XR=((4, NZ, nr, D), BF), ZS=((4, NZ, nr, D), BF), ZR=((4, NZ, nr, D), BF),
        NGS=((4, 8, D), F32), NGR=((3, 8, D), F32), NGZ=((NZ, 8, D), F32),
        SQ=((1, 1, 128), F32), SQS=((N, 1, 128), F32),
        FG=((NG, 4 * nr, D) if NG > 1 else (1, 16, 128), BF),
    )
    copies = dict(
        ids=1, gn=1, ex=NZ, ez=NZ, wu=3 * NZ, wd=3 * NZ, wx0=NZ, wx1=NZ, wx2=NZ, wx3=NZ, vu=2 * NZ, vd=2 * NZ, ay=NF, ac=2 * NF,
        h1=3, fc=2, fy=1, pool=1, df=3, bc=2, by=1, lx=TP, rx=TP, gx=4 * NZ, gz=4 * NZ, nc=1, ny=1, nx=1,
        nz=NZ, ff=3, fa=3, gg=2 * NG, sq=1, eu=2 * NZ, ed=2 * NZ, gex=NZ, gey=NZ, gez=2 * NZ, e1=1, e3=4, eg=NG,
    )
    return buffers, copies


def step_kernel(sizes, *refs):
    NR, NF, S, D, rows = sizes
    NX, NZ, NG = 2, NF // 2, NR // TP
    N, nr = NR * NF, D // NF
    HI = lax.Precision.HIGHEST
    buffers, copies = step_layout(sizes)
    given = (
        "length_in", "ids_in", "gn_in", "order_in", "labels_in", "cos_in", "sin_in", "pieces_in", "w_in",
        "ids_out", "ff_out", "fa_out", "ng_out", "stats_out", "ge_out",
    )
    v = types.SimpleNamespace(**dict(zip((*given, *buffers, "sids", "ssem", "rsem", "lsem"), refs, strict=True)))
    pool, W7, GW, DB, DQB, QKV = v.pool, v.W7, v.GW, v.DB, v.DQB, v.QKV
    ssem, rsem, lsem, ids_out, ge_out = v.ssem, v.rsem, v.lsem, v.ids_out, v.ge_out
    r = lax.axis_index("rep")
    f = lax.axis_index("fsdp")
    d = r * NF + f
    z, x = lax.div(f, NX), lax.rem(f, NX)
    g, t = lax.div(r, TP), lax.rem(r, TP)
    y, c = lax.div(t, 2), lax.rem(t, 2)
    ty = (1 - y) * 2 + c
    tc = y * 2 + 1 - c
    tyc = (1 - y) * 2 + 1 - c
    dev_x = (r, z * NX + 1 - x)
    dev_y = (g * TP + ty, f)
    dev_c = (g * TP + tc, f)

    GATE, UP, PT, PT2 = 0, 4 * S, 8 * S, 12 * S
    CR, CR2 = 16 * S, 18 * S
    H0F, H1F, HAT, DS2, DS1, DQ = 20 * S, 21 * S, 22 * S, 25 * S, 26 * S, 27 * S

    def blk(offset, index=0):
        return pl.ds(pl.multiple_of(offset + index * S, 128), S)

    sem_at, used = {}, 0
    for name, many in copies.items():
        sem_at[name] = used
        used += many
    later = []

    def copy(name, index, src, dst, dev, landing=None):
        base = sem_at[name]
        return pltpu.make_async_remote_copy(
            src_ref=src, dst_ref=dst, send_sem=ssem.at[base + index],
            recv_sem=rsem.at[base + (index if landing is None else landing)],
            device_id=dev, device_id_type=MESH,
        )

    def send(name, index, src, dst, dev, only=None, landing=None):
        def start():
            copy(name, index, src, dst, dev, landing).start()

        def finish():
            copy(name, index, src, dst, dev, landing).wait_send()

        if only is None:
            start()
            later.append(finish)
        else:
            pl.when(only)(start)
            later.append(lambda: pl.when(only)(finish))

    def arrive(name, index, dst, only=None):
        def wait():
            pltpu.make_async_copy(dst, dst, rsem.at[sem_at[name] + index]).wait()

        if only is None:
            wait()
        else:
            pl.when(only)(wait)

    def spread(name, src, dst):
        base = sem_at[name]

        def one(k, carry):
            to = lax.rem(d + k, N)
            pltpu.make_async_remote_copy(
                src_ref=src, dst_ref=dst.at[d], send_sem=ssem.at[base], recv_sem=rsem.at[base],
                device_id=(lax.div(to, NF), lax.rem(to, NF)), device_id_type=MESH,
            ).start()
            return carry

        lax.fori_loop(1, N, one, 0)
        rest = dst.at[pl.ds(0, N - 1)]
        later.append(lambda: pltpu.make_async_copy(rest, rest, ssem.at[base]).wait())

    def gather_all(name, dst):
        rest = dst.at[pl.ds(0, N - 1)]
        pltpu.make_async_copy(rest, rest, rsem.at[sem_at[name]]).wait()

    def keep(only, ref, at, value):
        @pl.when(only)
        def _():
            ref[at] = value

    def load(src, dst, sem):
        done = pltpu.make_async_copy(src, dst, lsem.at[sem])
        done.start()
        return done

    table = v.table if rows % 8 else pool.at[pl.ds(0, rows)]
    got_table = load(v.w_in, table, 0)
    slots = [t, 4, 5, 6]

    def wrow(index):
        return pl.ds(pl.multiple_of(index * nr, 16), nr)

    got_piece = [load(v.pieces_in.at[t, m], W7.at[slots[m], wrow(f)], 1 + m) for m in range(4)]
    got_ids = load(v.ids_in, ids_out.at[d], 5)
    v.GNB[f] = jnp.zeros((8, 128), F32)
    v.GNB[f, 0:6, 0:nr] = v.gn_in[...].astype(BF).astype(F32)
    barrier = pltpu.get_barrier_semaphore()

    def greet(k, carry):
        to = lax.rem(d + k, N)
        pl.semaphore_signal(
            barrier, inc=1, device_id=(lax.div(to, NF), lax.rem(to, NF)), device_id_type=MESH
        )
        return carry

    lax.fori_loop(1, N, greet, 0)
    got_ids.wait()
    for item in got_piece:
        item.wait()
    pl.semaphore_wait(barrier, N - 1)

    spread("ids", ids_out.at[d], ids_out)

    def piece(m, origin_z, origin_x):
        return W7.at[slots[m], wrow(origin_z * NX + origin_x)]

    def up_to(m, origin, only, which):
        here = piece(m, origin, which)
        if m < 3:
            send("wu", m * NZ + origin, here, here, (r, f + NX), only)
        else:
            send("vu", which * NZ + origin, here, here, (r, f + NX), only)

    def down_to(m, origin, only, which):
        here = piece(m, origin, which)
        if m < 3:
            send("wd", m * NZ + origin, here, here, (r, f - NX), only)
        else:
            send("vd", which * NZ + origin, here, here, (r, f - NX), only)

    def across(m, origin, only=None):
        here = piece(m, origin, x)
        send(f"wx{m}", origin, here, here, dev_x, only)

    def publish(index, only=None):
        here = W7.at[t, wrow(index)]
        send("ay", index, here, here, dev_y, only)
        send("ac", index, here, here, dev_c, only)

    def own_pieces(m):
        up_to(m, z, z + 1 < NZ, x)
        down_to(m, z, z >= 1, x)
        across(m, z)

    def relay(m, k):
        low, high = z - k, z + k
        below, above = jnp.maximum(low, 0), jnp.minimum(high, NZ - 1)
        for which in (x,) if m < 3 else (x, 1 - x):
            first = m * NZ if m < 3 else which * NZ
            arrive("wu" if m < 3 else "vu", first + below, piece(m, below, which), low >= 0)
            up_to(m, below, (low >= 0) & (z + 1 < NZ), which)
            if m < 3:
                across(m, below, low >= 0)
            if m == 0:
                publish(below * NX + x, low >= 0)
            arrive("wd" if m < 3 else "vd", first + above, piece(m, above, which), high < NZ)
            down_to(m, above, (high < NZ) & (z >= 1), which)
            if m < 3:
                across(m, above, high < NZ)
            if m == 0:
                publish(above * NX + x, high < NZ)

    own_pieces(0)
    publish(f)
    base_gn = sem_at["gn"]

    def gn_one(k, carry):
        pltpu.make_async_remote_copy(
            src_ref=v.GNB.at[f], dst_ref=v.GNB.at[f], send_sem=ssem.at[base_gn], recv_sem=rsem.at[base_gn],
            device_id=(r, lax.rem(f + k, NF)), device_id_type=MESH,
        ).start()
        return carry

    lax.fori_loop(1, NF, gn_one, 0)
    gn_rest = v.GNB.at[pl.ds(0, NF - 1)]
    later.append(lambda: pltpu.make_async_copy(gn_rest, gn_rest, ssem.at[base_gn]).wait())
    for m in (1, 2, 3):
        own_pieces(m)

    gather_all("ids", ids_out)
    got_sids = load(ids_out.at[pl.ds(pl.multiple_of(r * NF, NF), NF)], v.sids, 5)
    got_sids.wait()
    got_table.wait()
    start_row = f * rows
    EXS, EXO, EXR, EZR = (v.EX.at[i] for i in range(4))

    def rows_of(i, other):
        owner = i * NX + other

        def token(j, inner):
            wanted = v.sids[owner, 0, j] - start_row
            inside = (wanted >= 0) & (wanted < rows)
            row = table[pl.ds(jnp.clip(wanted, 0, rows - 1), 1), :]
            v.stage[pl.ds(j, 1), :] = jnp.where(inside, row, 0.0)
            return inner

        lax.fori_loop(0, S, token, 0, unroll=8)
        return v.stage[...].astype(BF)

    steps = [(m, k) for k in range(1, NZ) for m in (0, 1, 2, 3)]
    jobs = [(i, True) for i in range(NZ)] + [(i, False) for i in range(NZ)]
    at_step = 0
    for number, (i, away) in enumerate(jobs):
        if away:
            EXS[i] = rows_of(i, 1 - x)
            send("ex", i, EXS.at[i], EXR.at[i], dev_x)
        else:
            EXO[i] = rows_of(i, x)
        if number == 1:
            arrive("wx3", z, piece(3, z, 1 - x))
            up_to(3, z, z + 1 < NZ, 1 - x)
            down_to(3, z, z >= 1, 1 - x)
        while at_step < len(steps) * (number + 1) // (len(jobs) + 2) - 1:
            relay(*steps[at_step])
            at_step += 1

    for i in range(NZ):
        arrive("ex", i, EXR.at[i])
        total = EXO[i] + EXR[i]
        EXO[i] = total
        keep(z == i, EZR, i, total)
        send("ez", i, EXO.at[i], EZR.at[z], (r, i * NX + x), z != i, z)
    while at_step < len(steps):
        relay(*steps[at_step])
        at_step += 1

    for i in range(NZ):
        arrive("wx0", i, piece(0, i, 1 - x))
        publish(i * NX + 1 - x)
    for i in range(NF):
        there = W7.at[ty, wrow(i)]
        arrive("ay", i, there)
        send("ac", NF + i, there, there, dev_c)

    arrive("gn", 0, gn_rest)
    tiles = jnp.concatenate([v.GNB[i] for i in range(NF)], axis=1).astype(BF)
    at_row = lax.broadcasted_iota(jnp.int32, (NF * 128, D), 0)
    at_col = lax.broadcasted_iota(jnp.int32, (NF * 128, D), 1)
    lane = lax.bitwise_and(at_row, 127)
    pick = (lane < nr) & (lax.shift_right_logical(at_row, 7) * nr + lane == at_col)
    gains = dot(tiles, jnp.where(pick, 1.0, 0.0).astype(BF))
    gain = [gains[i : i + 1] for i in range(6)]

    for i in range(NZ):
        pl.when(z != i)(functools.partial(arrive, "ez", i, EZR.at[i]))
    embedded = EZR[0].astype(F32)
    for i in range(1, NZ):
        embedded = embedded + EZR[i].astype(F32)
    normed, hat, inverse = layer_norm(embedded, gain[0], gain[1])
    pool[blk(H0F), :] = normed
    pool[blk(HAT, 0), :] = hat
    v.INV[0] = inverse
    v.H0B[...] = normed.astype(BF)

    def to_rank(name, which, src, buffer):
        send(name, which, src, buffer.at[t], (g * TP + which, f), t != which, t)
        keep(t == which, buffer, which, src[...])

    for which in range(3):
        to_rank("lx", which, v.H0B, v.LX)

    for i in range(NF):
        arrive("ac", i, W7.at[tc, wrow(i)])
    for i in range(NF):
        arrive("ac", NF + i, W7.at[tyc, wrow(i)])
    tables = [jnp.concatenate([ref[...]] * (D // 128), axis=1) for ref in (v.cos_in, v.sin_in)]
    in_half = lax.bitwise_and(lax.broadcasted_iota(jnp.int32, (S, D), 1), HD - 1) < HD // 2

    def turn(values, sign):
        partner = jnp.where(
            in_half, pltpu.roll(values, D - HD // 2, 1), pltpu.roll(values, HD // 2, 1)
        )
        signed = jnp.where(in_half, -sign, sign) * tables[1]
        return values * tables[0] + partner * signed

    for j in range(3):
        projected = dot(v.H0B[...], W7[j])
        QKV[j] = (turn(projected, 1.0) if j < 2 else projected).astype(BF)
    length = v.length_in[0]
    allowed = lax.broadcasted_iota(jnp.int32, (1, S), 1) < length
    scaling = HD ** (-0.5)
    first_half = lax.broadcasted_iota(jnp.int32, (S, 128), 1) < HD

    def half(values, which):
        keep = first_half if which == 0 else jnp.logical_not(first_half)
        return jnp.where(keep, values, jnp.zeros_like(values))

    def attend(p, carry):
        lanes = pl.ds(pl.multiple_of(p * 128, 128), 128)
        query, keys, values = QKV[0, :, lanes], QKV[1, :, lanes], QKV[2, :, lanes]
        result = jnp.zeros((S, 128), F32)
        for which in range(2):
            scores = dot_nt(query, half(keys, which)) * scaling
            scores = jnp.where(allowed, scores, -1000000000.0)
            raised = jnp.exp(scores - jnp.max(scores, axis=-1, keepdims=True))
            chances = raised / jnp.sum(raised, axis=-1, keepdims=True)
            v.PS[2 * p + which] = chances
            result = result + dot(chances.astype(BF), half(values, which))
        v.ATT[:, lanes] = result.astype(BF)
        return carry

    lax.fori_loop(0, D // 128, attend, 0)
    branch = dot(v.ATT[...], W7[3])
    normed, hat, inverse = layer_norm(pool[blk(H0F), :] + branch, gain[2], gain[3])
    pool[blk(H1F), :] = normed
    pool[blk(HAT, 1), :] = hat
    v.INV[1] = inverse
    v.H1[t] = normed.astype(BF)

    def share(name, buffer):
        send(name, 0, buffer.at[t], buffer.at[t], dev_y)
        send(name, 1, buffer.at[t], buffer.at[t], dev_c)
        arrive(name, 0, buffer.at[ty])
        send(name, 2, buffer.at[ty], buffer.at[ty], dev_c)
        arrive(name, 1, buffer.at[tc])
        arrive(name, 2, buffer.at[tyc])

    def reduce(names, offset, landing, which):
        for i in range(2):
            send(names[0], i, pool.at[blk(offset, i * 2 + 1 - c)], pool.at[blk(landing, i)], dev_c)
        for i in range(2):
            arrive(names[0], i, pool.at[blk(landing, i)])
        away = pool[blk(offset, (1 - y) * 2 + c), :] + pool[blk(landing, 1 - y), :]
        v.YS[which] = away.astype(BF)
        send(names[1], 0, v.YS.at[which], v.YR.at[which], dev_y)
        mine = pool[blk(offset, t), :] + pool[blk(landing, y), :]
        arrive(names[1], 0, v.YR.at[which])
        return mine + v.YR[which].astype(F32)

    share("h1", v.H1)
    to_rank("lx", 3, v.ATT, v.LX)
    for m in range(1, 3):
        for i in range(NZ):
            arrive(f"wx{m}", i, piece(m, i, 1 - x))

    def forward(b, carry):
        gate, up = dot(v.H1[b], W7[4]), dot(v.H1[b], W7[5])
        pool[blk(GATE, b), :] = gate
        pool[blk(UP, b), :] = up
        mixed = (gate / (1.0 + jnp.exp(-gate)) * up).astype(BF)
        v.MIX[b] = mixed
        pool[blk(PT, b), :] = dot(mixed, W7[6])
        return carry

    lax.fori_loop(0, TP, forward, 0)
    feed = reduce(("fc", "fy"), PT, CR, 0)
    normed, hat, inverse = layer_norm(pool[blk(H1F), :] + feed, gain[4], gain[5])
    pool[blk(HAT, 2), :] = hat
    v.INV[2] = inverse
    present = jnp.where(lax.broadcasted_iota(jnp.int32, (S, 1), 0) < length, 1.0, 0.0)
    share_of = length.astype(F32)
    v.PROW[0] = jnp.sum(normed * present, axis=0, keepdims=True) / share_of

    spread("pool", v.PROW.at[0], v.PB)
    v.PB[d] = v.PROW[0]
    gather_all("pool", v.PB)
    for i in range(N):
        v.PM[pl.ds(i, 1), :] = v.PB[i]
    pooled = v.PM[...]
    wide = lax.broadcasted_iota(jnp.int32, (N, D), 1)
    row_at = lax.broadcasted_iota(jnp.int32, (N, N), 0)
    col_at = lax.broadcasted_iota(jnp.int32, (N, N), 1)
    order, labels = v.order_in[...].astype(F32), v.labels_in[...].astype(F32)

    def column(row):
        return jnp.sum(jnp.where(row_at == col_at, row, 0.0), axis=1, keepdims=True)

    slot_has = jnp.where(column(order) == col_at.astype(F32), 1.0, 0.0).astype(BF)
    label_is = jnp.where(column(labels) == order, 1.0, 0.0).astype(BF)
    paired = dot(slot_has, label_is)
    loss_value = jnp.zeros((1, 1), F32)
    d_pooled = jnp.zeros((N, D), F32)
    for width in (D // 12, D // 3, D):
        portion = jnp.where(wide < width, pooled, 0.0)
        inverse = lax.rsqrt(jnp.sum(portion * portion, axis=1, keepdims=True) + 1e-06)
        unit = portion * inverse
        similar = lax.dot_general(
            unit, unit, (((1,), (1,)), ((), ())), precision=HI, preferred_element_type=F32
        ) / logit_divisor
        similar = jnp.where(row_at == col_at, -1000000000.0, similar)
        row_max = jnp.max(similar, axis=1, keepdims=True)
        raised = jnp.exp(similar - row_max)
        total = jnp.sum(raised, axis=1, keepdims=True)
        target = jnp.sum(jnp.where(paired > 0.0, similar, 0.0), axis=1, keepdims=True)
        term = row_max + jnp.log(total) - target
        loss_value = loss_value + jnp.sum(term, axis=0, keepdims=True) / N
        col_max = jnp.max(similar, axis=0, keepdims=True)
        raised_t = jnp.exp(similar - col_max)
        turned = raised_t / jnp.sum(raised_t, axis=0, keepdims=True)
        d_similar = (raised / total + turned - 2.0 * paired) / (3.0 * N) / logit_divisor
        d_unit = lax.dot_general(
            d_similar, unit, (((1,), (0,)), ((), ())), precision=HI, preferred_element_type=F32
        )
        inner = jnp.sum(d_unit * unit, axis=1, keepdims=True)
        d_pooled = d_pooled + inverse * (d_unit - unit * inner)
    loss_value = loss_value / 3.0
    own_row = lax.broadcasted_iota(jnp.int32, (N, D), 0) == d
    d_mine = jnp.sum(jnp.where(own_row, d_pooled, 0.0), axis=0, keepdims=True)

    d_two = d_mine * present / share_of
    d_sum, d_gain_two, d_shift_two = norm_back(d_two, pool[blk(HAT, 2), :], v.INV[2], gain[4])
    pool[blk(DS2), :] = d_sum
    v.DF[t] = d_sum.astype(BF)
    share("df", v.DF)

    def back(b, carry):
        d_mixed = dot_nt(v.DF[b], W7[6])
        gate, up = pool[blk(GATE, b), :], pool[blk(UP, b), :]
        logistic = 1.0 / (1.0 + jnp.exp(-gate))
        d_gate = (d_mixed * up * (logistic * (1.0 + gate * (1.0 - logistic)))).astype(BF)
        d_up = (d_mixed * (gate * logistic)).astype(BF)
        v.DG[0, b] = d_gate
        v.DG[1, b] = d_up
        pool[blk(PT2, b), :] = dot_nt(d_gate, W7[4]) + dot_nt(d_up, W7[5])
        return carry

    TILE = 256

    def product(left, right, m):
        def tile(i, carry):
            at = pl.ds(pl.multiple_of(i * TILE, TILE), TILE)
            GW[m, at, :] = dot_tn(left(at), right()).astype(BF)
            return carry

        lax.fori_loop(0, D // TILE, tile, 0)

    def part(m, i, other):
        return GW.at[m, wrow(i * NX + other)]

    def give(m):
        for i in range(NZ):
            send("gx", m * NZ + i, part(m, i, 1 - x), v.XR.at[m, i], dev_x)

    def pass_on(m):
        for i in range(NZ):
            arrive("gx", m * NZ + i, v.XR.at[m, i])
            total = (part(m, i, x)[...].astype(F32) + v.XR[m, i].astype(F32)).astype(BF)
            v.ZS[m, i] = total
            keep(z == i, v.ZR, (m, i), total)
            send("gz", m * NZ + i, v.ZS.at[m, i], v.ZR.at[m, z], (r, i * NX + x), z != i, m * NZ + z)

    def product_rows(buffer):
        return lambda at: buffer[:, :, at].reshape(TP * S, TILE)

    product(product_rows(v.MIX), lambda: v.DF[...].reshape(TP * S, D), 3)
    give(3)
    lax.fori_loop(0, TP, back, 0)
    for i in range(2):
        send("bc", i, pool.at[blk(PT2, i * 2 + 1 - c)], pool.at[blk(CR2, i)], dev_c)
    product(product_rows(v.H1), lambda: v.DG[0].reshape(TP * S, D), 1)
    give(1)
    for i in range(2):
        arrive("bc", i, pool.at[blk(CR2, i)])
    away = pool[blk(PT2, (1 - y) * 2 + c), :] + pool[blk(CR2, 1 - y), :]
    v.YS[1] = away.astype(BF)
    send("by", 0, v.YS.at[1], v.YR.at[1], dev_y)
    product(product_rows(v.H1), lambda: v.DG[1].reshape(TP * S, D), 2)
    give(2)
    pass_on(3)
    mine = pool[blk(PT2, t), :] + pool[blk(CR2, y), :]
    arrive("by", 0, v.YR.at[1])
    d_one = pool[blk(DS2), :] + (mine + v.YR[1].astype(F32))

    d_sum, d_gain_one, d_shift_one = norm_back(d_one, pool[blk(HAT, 1), :], v.INV[1], gain[2])
    pool[blk(DS1), :] = d_sum
    DB[0] = d_sum.astype(BF)
    to_rank("rx", 3, DB.at[0], v.RX)
    DB[1] = dot_nt(DB[0], W7[3]).astype(BF)
    pass_on(1)

    def attend_back(p, carry):
        lanes = pl.ds(pl.multiple_of(p * 128, 128), 128)
        query, keys, values = QKV[0, :, lanes], QKV[1, :, lanes], QKV[2, :, lanes]
        grad = DB[1, :, lanes]
        d_query = jnp.zeros((S, 128), F32)
        d_keys = jnp.zeros((S, 128), F32)
        d_values = jnp.zeros((S, 128), F32)
        for which in range(2):
            chances = v.PS[2 * p + which]
            d_values = d_values + dot_tn(chances.astype(BF), half(grad, which))
            d_chances = dot_nt(grad, half(values, which))
            inner = jnp.sum(chances * d_chances, axis=-1, keepdims=True)
            d_scores = (chances * (d_chances - inner)).astype(BF)
            d_query = d_query + dot(d_scores, half(keys, which)) * scaling
            d_keys = d_keys + dot_tn(d_scores, half(query, which)) * scaling
        pool[blk(DQ, 0), lanes] = d_query
        pool[blk(DQ, 1), lanes] = d_keys
        DQB[2, :, lanes] = d_values.astype(BF)
        return carry

    lax.fori_loop(0, D // 128, attend_back, 0)
    for j in range(2):
        DQB[j] = turn(pool[blk(DQ, j), :], -1.0).astype(BF)

    for which in range(3):
        to_rank("rx", which, DQB.at[which], v.RX)
    d_zero = pool[blk(DS1), :]
    for j in range(3):
        d_zero = d_zero + dot_nt(DQB[j], W7[j])
    d_embedded, d_gain_zero, d_shift_zero = norm_back(d_zero, pool[blk(HAT, 0), :], v.INV[0], gain[0])
    DB[2] = d_embedded.astype(BF)

    got_own = load(DB.at[2], ge_out.at[d], 0)
    cut = D * 2 // 3
    cols = [pl.ds(0, cut), pl.ds(cut, D - cut)]

    def line(rep, which_x, order, i):
        return ge_out.at[rep * NF + i * NX + which_x, :, cols[order]]

    def all_of(rep, order):
        return ge_out.at[pl.ds(pl.multiple_of(rep * NF, NF), NF), :, cols[order]]

    def ge_up(order, origin, src, only):
        send("eu", order * NZ + origin, src, line(r, x, order, origin), (r, f + NX), only)

    def ge_down(order, origin, src, only):
        send("ed", order * NZ + origin, src, line(r, x, order, origin), (r, f - NX), only)

    for order in range(2):
        ge_up(order, z, DB.at[2, :, cols[order]], z + 1 < NZ)
        ge_down(order, z, DB.at[2, :, cols[order]], z >= 1)

    def ge_relay(k):
        low, high = z - k, z + k
        below, above = jnp.maximum(low, 0), jnp.minimum(high, NZ - 1)
        for order in range(2):
            arrive("eu", order * NZ + below, line(r, x, order, below), low >= 0)
            ge_up(order, below, line(r, x, order, below), (low >= 0) & (z + 1 < NZ))
            arrive("ed", order * NZ + above, line(r, x, order, above), high < NZ)
            ge_down(order, above, line(r, x, order, above), (high < NZ) & (z >= 1))

    v.NGS[0] = jnp.concatenate(
        [d_gain_zero, d_shift_zero, d_gain_one, d_shift_one, d_gain_two, d_shift_two,
         jnp.zeros((2, D), F32)], axis=0)
    stages = (("nc", dev_c), ("ny", dev_y), ("nx", dev_x))

    def norm_send(i):
        send(stages[i][0], 0, v.NGS.at[i], v.NGR.at[i], stages[i][1])

    def norm_add(i):
        arrive(stages[i][0], 0, v.NGR.at[i])
        v.NGS[i + 1] = v.NGS[i] + v.NGR[i]

    norm_send(0)
    pass_on(2)
    for which in range(TP):
        arrive("lx", which, v.LX.at[which], t != which)
        arrive("rx", which, v.RX.at[which], t != which)
    product(product_rows(v.LX), lambda: v.RX[...].reshape(TP * S, D), 0)
    give(0)
    norm_add(0)
    norm_send(1)
    got_own.wait()
    ge_relay(1)
    norm_add(1)
    norm_send(2)

    def settle(m, out, at):
        for i in range(NZ):
            arrive("gz", m * NZ + i, v.ZR.at[m, i], z != i)
        total = v.ZR[m, 0].astype(F32)
        for i in range(1, NZ):
            total = total + v.ZR[m, i].astype(F32)
        out[t, at, :] = total.astype(BF)

    def group_sum(out, first, size):
        own = v.FG.at[g, pl.ds(first, size)]
        own[...] = out[t]
        for k in range(1, NG):
            other = lax.rem(g + k, NG)
            index = (0 if first else NG) + k
            send("gg", index, own, own, (other * TP + t, f), None, (0 if first else NG) + g)
        for k in range(1, NG):
            other = lax.rem(g + k, NG)
            arrive("gg", (0 if first else NG) + other, v.FG.at[other, pl.ds(first, size)])
        total = v.FG[0, pl.ds(first, size)].astype(F32)
        for k in range(1, NG):
            total = total + v.FG[k, pl.ds(first, size)].astype(F32)
        out[t] = total.astype(BF)

    settle(3, v.ff_out, pl.ds(2 * nr, nr))
    settle(1, v.ff_out, pl.ds(0, nr))
    for k in range(2, NZ):
        ge_relay(k)
    norm_add(2)
    for i in range(NZ):
        send("nz", i, v.NGS.at[3], v.NGZ.at[z], (r, i * NX + x), z != i, z)
        keep(z == i, v.NGZ, i, v.NGS[3])
    for i in range(NZ):
        here = line(r, x, 0, i)
        send("gex", i, here, here, dev_x)
    for i in range(NZ):
        here = line(r, x, 1, i)
        send("gey", i, here, here, dev_y)
    pass_on(0)
    settle(2, v.ff_out, pl.ds(nr, nr))
    if NG > 1:
        group_sum(v.ff_out, nr, 3 * nr)
    own = v.ff_out[t].astype(F32)
    squares = jnp.sum(own * own)
    ry, rc, ryc = g * TP + ty, g * TP + tc, g * TP + tyc
    for i in range(NZ):
        arrive("gex", i, line(r, 1 - x, 0, i))
    send("e1", 0, all_of(r, 0), all_of(r, 0), dev_y)
    send("e3", 0, all_of(r, 0), all_of(r, 0), dev_c)
    for i in range(NZ):
        arrive("gey", i, line(ry, x, 1, i))
    for i in range(NZ):
        for which, rep in enumerate((r, ry)):
            here = line(rep, x, 1, i)
            send("gez", which * NZ + i, here, here, dev_x)
    share("ff", v.ff_out)
    settle(0, v.fa_out, pl.ds(0, nr))
    if NG > 1:
        group_sum(v.fa_out, 0, nr)
    own = v.fa_out[t].astype(F32)
    squares = squares + jnp.sum(own * own)
    squares = jnp.where(g == 0, squares, 0.0)
    share("fa", v.fa_out)

    for i in range(NZ):
        arrive("nz", i, v.NGZ.at[i], z != i)
    total_norms = v.NGZ[0]
    for i in range(1, NZ):
        total_norms = total_norms + v.NGZ[i]
    arrive("e1", 0, all_of(ry, 0))
    send("e3", 1, all_of(ry, 0), all_of(ry, 0), dev_c)
    for i in range(NZ):
        for which, rep in enumerate((r, ry)):
            arrive("gez", which * NZ + i, line(rep, 1 - x, 1, i))
    send("e3", 2, all_of(r, 1), all_of(r, 1), dev_c)
    send("e3", 3, all_of(ry, 1), all_of(ry, 1), dev_c)
    for which, (rep, order) in enumerate(((rc, 0), (ryc, 0), (rc, 1), (ryc, 1))):
        arrive("e3", which, all_of(rep, order))
    if NG > 1:

        def group(which):
            return ge_out.at[pl.ds(pl.multiple_of(which * TP * NF, TP * NF), TP * NF)]

        for k in range(1, NG):
            other = lax.rem(g + k, NG)
            send("eg", k, group(g), group(g), (other * TP + t, f), None, g)
        for k in range(1, NG):
            other = lax.rem(g + k, NG)
            arrive("eg", other, group(other))

    def fetch(b):
        return pltpu.make_async_copy(
            ge_out.at[pl.ds(b * NZ, NZ)], v.EX.at[2 + lax.rem(b, 2)], lsem.at[1 + lax.rem(b, 2)]
        )

    fetch(0).start()
    same = lax.broadcasted_iota(jnp.int32, (S, S), 0) == lax.broadcasted_iota(jnp.int32, (S, S), 1)
    own_ids = jnp.sum(
        jnp.where(same, ids_out[d, :, pl.ds(0, S)].astype(F32), 0.0), axis=1, keepdims=True
    )

    def pairs_of(b, carry):
        pl.when(b + 1 < N // NZ)(lambda: fetch(b + 1).start())
        fetch(b).wait()
        for i in range(NZ):
            both = dot_nt(DB[2], v.EX[2 + lax.rem(b, 2), i])
            theirs = ids_out[b * NZ + i, :, pl.ds(0, S)].astype(F32)
            carry = carry + jnp.where(own_ids == theirs, both, 0.0)
        return carry

    both = lax.fori_loop(0, N // NZ, pairs_of, jnp.zeros((S, S), F32))
    squares = squares + jnp.sum(both)
    squares = squares + jnp.where(d == 0, jnp.sum(total_norms * total_norms), 0.0)
    v.SQ[0] = jnp.zeros((1, 128), F32) + squares
    spread("sq", v.SQ.at[0], v.SQS)
    v.SQS[d] = v.SQ[0]
    v.ng_out[...] = total_norms
    gather_all("sq", v.SQS)
    all_squares = v.SQS[0]
    for i in range(1, N):
        all_squares = all_squares + v.SQS[i]
    v.stats_out[...] = jnp.concatenate(
        [jnp.zeros((1, 128), F32) + loss_value, jnp.sqrt(all_squares), jnp.zeros((6, 128), F32)], axis=0
    )
    for finish in later:
        finish()


def run_step(sizes, *args):
    NR, NF, S, D, rows = sizes
    N, nr = NR * NF, D // NF
    vmem = pl.BlockSpec(memory_space=pltpu.VMEM)
    smem = pl.BlockSpec(memory_space=pltpu.SMEM)
    hbm = pl.BlockSpec(memory_space=pl.ANY)
    buffers, copies = step_layout(sizes)
    many = sum(copies.values())
    return pl.pallas_call(
        functools.partial(step_kernel, sizes),
        name="step",
        out_shape=(
            jax.ShapeDtypeStruct((N, 1, 2 * S), jnp.int32),
            jax.ShapeDtypeStruct((TP, 3 * nr, D), BF),
            jax.ShapeDtypeStruct((TP, nr, D), BF),
            jax.ShapeDtypeStruct((8, D), F32),
            jax.ShapeDtypeStruct((8, 128), F32),
            jax.ShapeDtypeStruct((N, S, D), BF),
        ),
        in_specs=[smem] + [vmem] * 6 + [hbm] * 2,
        out_specs=(vmem,) * 5 + (hbm,),
        scratch_shapes=[pltpu.VMEM(*item) for item in buffers.values()]
        + [
            pltpu.SMEM((NF, 1, 2 * S), jnp.int32), pltpu.SemaphoreType.DMA((many,)),
            pltpu.SemaphoreType.DMA((many,)), pltpu.SemaphoreType.DMA((8,)),
        ],
        compiler_params=pltpu.CompilerParams(
            collective_id=0, has_side_effects=True, vmem_limit_bytes=67_000_000
        ),
    )(*args)


def adamw(weight, grad, first, second, rate):
    first_new = beta_first * first + (1.0 - beta_first) * grad
    second_new = beta_second * second + (1.0 - beta_second) * grad * grad
    first_fix = 1.0 - beta_first**STEP
    second_fix = 1.0 - beta_second**STEP
    update = first_new / first_fix / (jnp.sqrt(second_new / second_fix) + adam_floor)
    return (weight - rate * (update + weight_decay * weight), first_new, second_new)


CHUNK, SLOTS = 424, 6


def finish_kernel(sizes, *refs):
    NR, NF, S, D, rows = sizes
    N, nr = NR * NF, D // NF
    names = ("ids", "ge", "ff", "fa", "norms", "stats", "pw", "pm", "pv") + tuple(
        f"{kind}{which}" for kind in "eaogd" for which in range(3)
    )
    results = ("qw", "qm", "qv") + tuple(f"{kind}{which}_new" for kind in "eaogd" for which in range(3))
    scratch = (
        "grads", "landing", "stage", "TB", "LA", "LO", "LG", "LD", "row_of", "token_of", "first_of", "sems",
        "ins", "outs", "tin", "tout",
    )
    v = types.SimpleNamespace(**dict(zip((*names, *results, *scratch), refs, strict=True)))
    start_row = lax.axis_index("fsdp") * rows
    n_chunks = rows // CHUNK

    def fetch(s):
        return pltpu.make_async_copy(v.ge.at[s], v.landing.at[lax.rem(s, 4)], v.sems.at[lax.rem(s, 4)])

    for s in range(3):
        fetch(s).start()
    layers = (("a", v.LA), ("o", v.LO), ("d", v.LD), ("g", v.LG))

    def layer(index, inward):
        kind, buffer = layers[index]
        for which in range(3):
            if inward:
                yield pltpu.make_async_copy(
                    getattr(v, f"{kind}{which}"), buffer.at[which], v.ins.at[index * 3 + which]
                )
            else:
                yield pltpu.make_async_copy(
                    buffer.at[which], getattr(v, f"{kind}{which}_new"), v.outs.at[index * 3 + which]
                )

    def chunk(k, inward):
        at, slot = pl.ds(k * CHUNK, CHUNK), k % SLOTS
        for which in range(3):
            old, new = getattr(v, f"e{which}"), getattr(v, f"e{which}_new")
            if inward:
                yield pltpu.make_async_copy(old.at[at], v.TB.at[slot, which], v.tin.at[slot, which])
            else:
                yield pltpu.make_async_copy(v.TB.at[slot, which], new.at[at], v.tout.at[slot, which])

    for index in range(4):
        for item in layer(index, True):
            item.start()
    for k in range(min(SLOTS, n_chunks)):
        for item in chunk(k, True):
            item.start()

    factor = jnp.minimum(1.0, clip_level / (v.stats[1:2, 0:1] + 1e-06))

    def apply(buffer, at, grad):
        index = tuple(at)
        new = adamw(
            buffer[(0, *index)], grad * factor, buffer[(1, *index)], buffer[(2, *index)], learn_rate
        )
        for which in range(3):
            buffer[(which, *index)] = new[which]

    def finish_layer(index):
        for item in layer(index, False):
            item.start()

    whole = pl.ds(0, nr)
    for item in layer(0, True):
        item.wait()
    for q in range(3):
        apply(v.LA, (whole, pl.ds(q * D, D)), v.fa[q].astype(F32))
    finish_layer(0)
    for item in layer(1, True):
        item.wait()
    apply(v.LO, (whole, pl.ds(0, D)), v.fa[3].astype(F32))
    finish_layer(1)
    for item in layer(2, True):
        item.wait()

    def down(q, carry):
        at = pl.ds(pl.multiple_of(q * nr, 16), nr)
        apply(v.LD, (at, pl.ds(0, D)), v.ff[q, pl.ds(2 * nr, nr), :].astype(F32))
        return carry

    lax.fori_loop(0, TP, down, 0)
    finish_layer(2)
    for item in layer(3, True):
        item.wait()
    quarter, span = D // TP, 2 * D // 6
    at_row = lax.broadcasted_iota(jnp.int32, (span, D), 0)
    at_col = lax.broadcasted_iota(jnp.int32, (span, D), 1)
    group = lax.div(at_col, nr)
    unit = lax.div(group, TP) * nr + (at_col - group * nr)
    holder = lax.rem(group, TP)
    for b in range(TP):
        first = quarter * b // 128 * 128
        total = jnp.zeros((2 * nr, D), F32)
        for q in range(TP):
            pick = (at_row + (first - quarter * b) == unit) & (holder == q)
            total = total + dot(
                v.ff[q, pl.ds(0, 2 * nr), pl.ds(first, span)], jnp.where(pick, 1.0, 0.0).astype(BF)
            )
        apply(v.LG, (whole, pl.ds(b * D, D)), total[:nr])
        apply(v.LG, (whole, pl.ds((TP + b) * D, D)), total[nr:])
    finish_layer(3)
    at_row = lax.broadcasted_iota(jnp.int32, (D, 128), 0)
    at_col = lax.broadcasted_iota(jnp.int32, (D, 128), 1)
    pick = (at_row - lax.axis_index("fsdp") * nr == at_col) & (at_col < nr)
    mine = lax.dot_general(
        v.norms[...], jnp.where(pick, 1.0, 0.0), (((1,), (0,)), ((), ())),
        precision=lax.Precision.HIGHEST, preferred_element_type=F32,
    )
    v.qw[...], v.qm[...], v.qv[...] = adamw(
        v.pw[...], mine[:6, :nr] * factor, v.pm[...], v.pv[...], norm_rate
    )

    def clear(i, carry):
        v.grads[pl.ds(pl.multiple_of(i * CHUNK, 8), CHUNK), :] = jnp.zeros((CHUNK, D), F32)
        return carry

    lax.fori_loop(0, n_chunks, clear, 0)

    def scan(s, count):
        v.first_of[s] = count

        def eight(b, inner):
            for i in range(8):
                j = b * 8 + i
                row = v.ids[s, 0, j] - start_row
                inside = (row >= 0) & (row < rows)
                v.row_of[inner] = row
                v.token_of[inner] = j
                inner = inner + inside.astype(jnp.int32)
            return inner

        return lax.fori_loop(0, lax.shift_right_logical(v.ids[s, 0, S] + 7, 3), eight, count)

    v.first_of[N] = lax.fori_loop(0, N, scan, 0)

    def sequence(s, carry):
        pl.when(s + 3 < N)(lambda: fetch(s + 3).start())
        fetch(s).wait()
        v.stage[...] = v.landing[lax.rem(s, 4)].astype(F32)

        def token(k, inner):
            at = pl.ds(v.row_of[k], 1)
            v.grads[at, :] = v.grads[at, :] + v.stage[pl.ds(v.token_of[k], 1), :]
            return inner

        return lax.fori_loop(v.first_of[s], v.first_of[s + 1], token, carry)

    lax.fori_loop(0, N, sequence, 0)

    for k in range(n_chunks):
        for item in chunk(k, True):
            item.wait()
        slot = k % SLOTS

        def part(first, size, k=k, slot=slot):
            at = pl.ds(pl.multiple_of(k * CHUNK + first, 8), size)
            grad = v.grads[at, :]
            apply(v.TB.at[slot], (pl.ds(pl.multiple_of(first, 8), size), pl.ds(0, D)), grad)

        def tile(i, carry, part=part):
            part(i * 32, 32)
            return carry

        lax.fori_loop(0, CHUNK // 32, tile, 0)
        if CHUNK % 32:
            part(CHUNK // 32 * 32, CHUNK % 32)
        for item in chunk(k, False):
            item.start()
        if k >= 1 and k - 1 + SLOTS < n_chunks:
            for item in chunk(k - 1, False):
                item.wait()
            for item in chunk(k - 1 + SLOTS, True):
                item.start()
    for k in range(n_chunks):
        if k + SLOTS >= n_chunks or k == n_chunks - 1:
            for item in chunk(k, False):
                item.wait()
    for index in range(4):
        for item in layer(index, False):
            item.wait()


def finish(sizes, ids, ge, ff, fa, norms, stats, norm_state, states):
    NR, NF, S, D, rows = sizes
    N, nr = NR * NF, D // NF
    hbm = pl.BlockSpec(memory_space=pl.ANY)
    vmem = pl.BlockSpec(memory_space=pltpu.VMEM)
    smem = pl.BlockSpec(memory_space=pltpu.SMEM)
    flat = [item for state in states for item in state]
    shapes = [jax.ShapeDtypeStruct(item.shape, F32) for item in (*norm_state, *flat)]
    return pl.pallas_call(
        functools.partial(finish_kernel, sizes),
        name="finish",
        out_shape=tuple(shapes),
        in_specs=[smem, hbm] + [vmem] * 7 + [hbm] * 15,
        out_specs=(vmem,) * 3 + (hbm,) * 15,
        scratch_shapes=[
            pltpu.VMEM((rows, D), F32), pltpu.VMEM((4, S, D), BF), pltpu.VMEM((S, D), F32),
            pltpu.VMEM((SLOTS, 3, CHUNK, D), F32),
            pltpu.VMEM((3, nr, 3 * D), F32), pltpu.VMEM((3, nr, D), F32), pltpu.VMEM((3, nr, 8 * D), F32),
            pltpu.VMEM((3, 4 * nr, D), F32),
            pltpu.SMEM((N * S + 8,), jnp.int32), pltpu.SMEM((N * S + 8,), jnp.int32),
            pltpu.SMEM((N + 1,), jnp.int32), pltpu.SemaphoreType.DMA((4,)), pltpu.SemaphoreType.DMA((12,)),
            pltpu.SemaphoreType.DMA((12,)), pltpu.SemaphoreType.DMA((SLOTS, 3)),
            pltpu.SemaphoreType.DMA((SLOTS, 3)),
        ],
        compiler_params=pltpu.CompilerParams(vmem_limit_bytes=62_000_000),
    )(ids, ge, ff, fa, norms, stats, *norm_state, *flat)


def table_kernel(sizes, ids, ge, factor, w, m, v, w_out, m_out, v_out, grads, landing, stage, sems):
    NR, NF, S, D, rows = sizes
    N = NR * NF
    step = pl.program_id(0)
    block = w.shape[0]

    @pl.when(step == 0)
    def _():
        start_row = lax.axis_index("fsdp") * rows

        def fetch(s):
            return pltpu.make_async_copy(ge.at[s], landing.at[lax.rem(s, 4)], sems.at[lax.rem(s, 4)])

        for s in range(3):
            fetch(s).start()

        def clear(i, carry):
            grads[pl.ds(pl.multiple_of(i * block, 8), block), :] = jnp.zeros((block, D), F32)
            return carry

        lax.fori_loop(0, grads.shape[0] // block, clear, 0)

        def sequence(s, carry):
            pl.when(s + 3 < N)(lambda: fetch(s + 3).start())
            fetch(s).wait()
            stage[...] = landing[lax.rem(s, 4)].astype(F32)

            def token(j, inner):
                wanted = ids[s, 0, j] - start_row

                @pl.when((wanted >= 0) & (wanted < rows))
                def _():
                    at = pl.ds(wanted, 1)
                    grads[at, :] = grads[at, :] + stage[pl.ds(j, 1), :]

                return inner

            return lax.fori_loop(0, S, token, carry)

        lax.fori_loop(0, N, sequence, 0)

    grad = grads[pl.ds(pl.multiple_of(step * block, 8), block), :] * factor[0:1, 0:1]
    w_out[...], m_out[...], v_out[...] = adamw(w[...], grad, m[...], v[...], learn_rate)


def update_table(sizes, ids, ge, factor, w, m, v):
    NR, NF, S, D, rows = sizes
    block = 424
    steps = pl.cdiv(rows, block)
    part = pl.BlockSpec((block, D), lambda i: (i, 0))
    return pl.pallas_call(
        functools.partial(table_kernel, sizes),
        name="table",
        grid=(steps,),
        out_shape=(jax.ShapeDtypeStruct((rows, D), F32),) * 3,
        in_specs=[
            pl.BlockSpec(memory_space=pltpu.SMEM), pl.BlockSpec(memory_space=pl.ANY),
            pl.BlockSpec((8, 128), lambda i: (0, 0)), part, part, part,
        ],
        out_specs=(part, part, part),
        scratch_shapes=[
            pltpu.VMEM((steps * block, D), F32), pltpu.VMEM((4, S, D), BF), pltpu.VMEM((S, D), F32),
            pltpu.SemaphoreType.DMA((4,)),
        ],
        compiler_params=pltpu.CompilerParams(vmem_limit_bytes=60_000_000),
    )(ids, ge, factor, w, m, v)


def local(
    sizes,
    token_ids,
    lengths,
    slot_order,
    pair_labels,
    embedding,
    attend_weight,
    attention_output_matrix,
    gate_up,
    contract_kernel,
    norm_params,
    embedding_first,
    embedding_second,
    attend_first,
    attend_second,
    output_first,
    output_second,
    gate_up_first,
    gate_up_second,
    down_first,
    down_second,
    norm_first,
    norm_second,
):
    NR, NF, S, D, rows = sizes
    nr = D // NF
    f = lax.axis_index("fsdp")
    N = NR * NF
    positions = jnp.arange(S)
    angles = (
        positions.astype(F32)[:, None]
        * (1000.0 ** (-2.0 * jnp.arange(HD // 2).astype(F32) / HD))[None, :]
    )
    cosine, sine = jnp.tile(jnp.cos(angles), (1, 128 * 2 // HD)), jnp.tile(jnp.sin(angles), (1, 128 * 2 // HD))
    attention = jnp.concatenate(
        [attend_weight.reshape(nr, 3, D).transpose(1, 0, 2), attention_output_matrix[None]], axis=0
    ).astype(BF)
    hidden = gate_up.astype(BF).reshape(nr, 2, NF, TP, nr).transpose(3, 1, 0, 2, 4).reshape(TP, 2, nr, D)
    down = contract_kernel.astype(BF).reshape(TP, 1, nr, D)
    pieces = jnp.concatenate([attention[:, None], hidden, down], axis=1)
    ids, ffn, att, norms, stats, ge = run_step(
        sizes,
        lengths,
        jnp.concatenate([token_ids, jnp.broadcast_to(lengths[:, None], (1, S))], axis=1),
        norm_params,
        slot_order.reshape(1, N),
        pair_labels.reshape(1, N),
        cosine,
        sine,
        pieces,
        embedding,
    )
    loss_value, grad_norm = stats[0, 0], stats[1, 0]
    if rows % CHUNK == 0:
        norm_next, *rest = split_three(
            finish(
                sizes, ids, ge, ffn, att, norms, stats, (norm_params, norm_first, norm_second),
                (
                    (embedding, embedding_first, embedding_second),
                    (attend_weight, attend_first, attend_second),
                    (attention_output_matrix, output_first, output_second),
                    (gate_up, gate_up_first, gate_up_second),
                    (contract_kernel, down_first, down_second),
                ),
            )
        )
        return (loss_value, grad_norm, *(item for state in rest for item in state), *norm_next)
    factor = jnp.minimum(1.0, clip_level / (grad_norm + 1e-06))
    factor_tile = jnp.broadcast_to(factor, (8, 128))
    emb_next = update_table(sizes, ids, ge, factor_tile, embedding, embedding_first, embedding_second)
    fin = ffn.reshape(TP, 3, nr, D)
    grad_attend = att[:3].transpose(1, 0, 2).reshape(nr, 3 * D).astype(F32)
    grad_output = att[3].astype(F32)
    grad_hidden = (
        fin[:, :2].reshape(TP, 2, nr, NF, nr).transpose(2, 1, 3, 0, 4).reshape(nr, 8 * D).astype(F32)
    )
    grad_down = fin[:, 2].reshape(TP * nr, D).astype(F32)
    grad_norms = lax.dynamic_slice(norms, (0, f * nr), (6, nr))
    att_next = adamw(attend_weight, grad_attend * factor, attend_first, attend_second, learn_rate)
    out_next = adamw(
        attention_output_matrix, grad_output * factor, output_first, output_second, learn_rate
    )
    gate_next = adamw(gate_up, grad_hidden * factor, gate_up_first, gate_up_second, learn_rate)
    down_next = adamw(contract_kernel, grad_down * factor, down_first, down_second, learn_rate)
    norm_next = adamw(norm_params, grad_norms * factor, norm_first, norm_second, norm_rate)
    return (
        loss_value, grad_norm, *emb_next, *att_next, *out_next, *gate_next, *down_next, *norm_next
    )


def split_three(flat):
    return [flat[i : i + 3] for i in range(0, len(flat), 3)]


def solution(mesh):
    NR, NF = mesh.shape["rep"], mesh.shape["fsdp"]
    rows_spec, cols_spec = P("fsdp", None), P(None, "fsdp")

    def step(*args):
        S, D, rows = args[0].shape[1], args[4].shape[1], args[4].shape[0] // NF
        run = jax.shard_map(
            functools.partial(local, (NR, NF, S, D, rows)),
            mesh=mesh,
            in_specs=(P(("rep", "fsdp"), None), P(("rep", "fsdp")), P(), P())
            + (rows_spec,) * 5 + (cols_spec,) + (rows_spec,) * 10 + (cols_spec,) * 2,
            out_specs=(P(), P()) + (rows_spec,) * 15 + (cols_spec,) * 3,
            check_vma=False,
        )
        return run(*args)

    return step
```

time: 424 us -> 338 us (0.80)
  Pallas kernels: 368 us -> 323 us
  other arithmetic: 28.2 us -> 5 us
  local copies, waits for them, and re-layouts: 24.4 us -> 7.27 us
    pallas_call x1, Pallas kernels: 105 us -> 59.8 us  [finish(): pl.pallas_call(functools.partial(finish_kernel, sizes), name='finish', ou...]
    sub x5 -> x0, other arithmetic: 16.3 us -> none  [adamw(): weight - rate * (update + weight_decay * weight)]
    mul x4 -> x0, local copies, waits for them, and re-layouts: 12.2 us -> none  [the longest x3 12.1 us: local(): grad_hidden * factor]
where the time goes in v2:
time: 338 us; the launch traced here: 337 us
  Pallas kernels  323 us (96%)
  local copies, waits for them, and re-layouts  7.27 us (2%)
  other arithmetic  5 us (1%)
    pallas_call x1, Pallas kernels, run_step(): pl.pallas_call(functools.partial(step_kernel, sizes), name='step', out_sh...  263 us
    pallas_call x1, Pallas kernels, finish(): pl.pallas_call(functools.partial(finish_kernel, sizes), name='finish', ou...  59.8 us

profile of v2, /device:TPU:0, one launch (start us, length us, event | category | flops | bytes accessed | tf_op | source)
XLA Modules:
  0.0 336.9 jit_solution(3186682487832992317)
XLA Ops:
  0.7 0.1 multiply_sine_fusion
  0.8 0.7 copy.45.refs_5_
  1.6 0.7 copy.46.refs_6_
  3.0 1.2 concatenate.21.refs_1_
  4.2 1.8 convert_element_type.34
  6.0 1.6 reshape.166
  7.6 0.2 copy.50
  7.8 1.3 reshape.167
  9.1 0.0 copy-start
  9.1 0.0 copy-start.1
  9.2 1.3 convert.10
  10.5 0.1 copy-done
  10.7 0.1 convert_element_type.35
  10.7 0.0 copy-done.1
  10.8 1.6 pad_maximum_fusion.refs_7_
  12.4 263.4 %step.1 = (s32[32,1,256]{2,1,0:T(1,128)}, bf16[4,288,768]{2,1,0:T(8,128)(2,1)}, bf16[4,96,768]{2,1,0:T(8,128)(2,1)}, f32[8,768]{1,0:T(8,128)}, f32[8,128]{1,0:T(8,128)}, /*index=5*/bf16[32,128,768]{2,1,0:T(8,128)(2,1)}) custom-call(s32[1]{0:T(128)} %copy.52.refs_0_, s32[1,256]{1,0:T(1,128)} %concatenate.21.refs_1_, f32[6,96]{1,0:T(8,128)} %refs_6_.1, ...), custom_call_target="tpu_custom_call" | custom-call | tf_op jit(solution)/shard_map/step/pallas_call | solution.py:799
  275.8 59.8 %finish.1 = (f32[6,96]{1,0:T(8,128)}, f32[6,96]{1,0:T(8,128)}, f32[6,96]{1,0:T(8,128)}, f32[3816,768]{1,0:T(8,128)}, f32[3816,768]{1,0:T(8,128)}, /*index=5*/f32...) custom-call(s32[32,1,256]{2,1,0:T(1,128)} %get-tuple-element.45.refs, ...), custom_call_target="tpu_custom_call" | custom-call | tf_op jit(solution)/shard_map/finish/pallas_call | solution.py:1027
  335.6 1.3 fusion
  (6 shorter events, 0.1 us)
Async XLA Ops:
  9.1 1.5 copy-start
  9.1 1.6 copy-start.1

commit v3 on v2

--- a/solution.py
+++ b/solution.py
@@ -80,12 +80,14 @@
         XR=((4, NZ, nr, D), BF), ZS=((4, NZ, nr, D), BF), ZR=((4, NZ, nr, D), BF),
         NGS=((4, 8, D), F32), NGR=((3, 8, D), F32), NGZ=((NZ, 8, D), F32),
         SQ=((1, 1, 128), F32), SQS=((N, 1, 128), F32),
+        PA=((nr, D), F32), PD=((nr, D), F32), PG=((nr, 8 * D), F32), IDF=((N, S), F32), RANK=((2, N, S), F32),
         FG=((NG, 4 * nr, D) if NG > 1 else (1, 16, 128), BF),
     )
     copies = dict(
         ids=1, gn=1, ex=NZ, ez=NZ, wu=3 * NZ, wd=3 * NZ, wx0=NZ, wx1=NZ, wx2=NZ, wx3=NZ, vu=2 * NZ, vd=2 * NZ, ay=NF, ac=2 * NF,
         h1=3, fc=2, fy=1, pool=1, df=3, bc=2, by=1, lx=TP, rx=TP, gx=4 * NZ, gz=4 * NZ, nc=1, ny=1, nx=1,
-        nz=NZ, ff=3, fa=3, gg=2 * NG, sq=1, eu=2 * NZ, ed=2 * NZ, gex=NZ, gey=NZ, gez=2 * NZ, e1=1, e3=4, eg=NG,
+        nz=NZ, ff=3, fa=3, gg=2 * NG, sq=1, eu=2 * NZ, ed=2 * NZ, e0x=NZ, e0y=NF, e0c=2 * NF, e1x=2 * NZ, e1y=NZ,
+        e1c=2 * NF, eg=NG,
     )
     return buffers, copies
 
@@ -97,8 +99,8 @@
     HI = lax.Precision.HIGHEST
     buffers, copies = step_layout(sizes)
     given = (
-        "length_in", "ids_in", "gn_in", "order_in", "labels_in", "cos_in", "sin_in", "pieces_in", "w_in",
-        "ids_out", "ff_out", "fa_out", "ng_out", "stats_out", "ge_out",
+        "length_in", "ids_in", "gn_in", "order_in", "labels_in", "cos_in", "sin_in", "qkv_in", "o_in", "gu_in", "down_in",
+        "w_in", "ids_out", "ff_out", "fa_out", "ng_out", "stats_out", "list_out", "ge_out",
     )
     v = types.SimpleNamespace(**dict(zip((*given, *buffers, "sids", "ssem", "rsem", "lsem"), refs, strict=True)))
     pool, W7, GW, DB, DQB, QKV = v.pool, v.W7, v.GW, v.DB, v.DQB, v.QKV
@@ -190,14 +192,25 @@
         return done
 
     table = v.table if rows % 8 else pool.at[pl.ds(0, rows)]
-    got_table = load(v.w_in, table, 0)
     slots = [t, 4, 5, 6]
 
     def wrow(index):
         return pl.ds(pl.multiple_of(index * nr, 16), nr)
 
-    got_piece = [load(v.pieces_in.at[t, m], W7.at[slots[m], wrow(f)], 1 + m) for m in range(4)]
-    got_ids = load(v.ids_in, ids_out.at[d], 5)
+    got_gate = load(v.gu_in, v.PG, 1)
+    got_down = load(v.down_in.at[wrow(t)], v.PD, 2)
+
+    @pl.when(t < 3)
+    def _():
+        load(v.qkv_in.at[:, pl.ds(pl.multiple_of(jnp.minimum(t, 2) * D, 128), D)], v.PA, 3)
+
+    @pl.when(t == 3)
+    def _():
+        load(v.o_in, v.PA, 3)
+
+    length = v.length_in[0]
+    ids_out[d, :, pl.ds(0, S)] = v.ids_in[...]
+    ids_out[d, :, pl.ds(S, S)] = jnp.zeros((1, S), jnp.int32) + length
     v.GNB[f] = jnp.zeros((8, 128), F32)
     v.GNB[f, 0:6, 0:nr] = v.gn_in[...].astype(BF).astype(F32)
     barrier = pltpu.get_barrier_semaphore()
@@ -210,9 +223,31 @@
         return carry
 
     lax.fori_loop(1, N, greet, 0)
-    got_ids.wait()
-    for item in got_piece:
-        item.wait()
+    pltpu.make_async_copy(v.o_in, v.PA, lsem.at[3]).wait()
+    W7[t, wrow(f), :] = v.PA[...].astype(BF)
+    got_down.wait()
+    W7[6, wrow(f), :] = v.PD[...].astype(BF)
+    got_gate.wait()
+    got_table = load(v.w_in, table, 0)
+    quarter, span = D // TP, D // 3
+    unit_row = lax.broadcasted_iota(jnp.int32, (D, span), 0)
+    unit_col = lax.broadcasted_iota(jnp.int32, (D, span), 1)
+    unit_group = lax.div(unit_row, nr)
+    unit_at = lax.div(unit_group, TP) * nr + (unit_row - unit_group * nr)
+    unit_mine = lax.rem(unit_group, TP) == t
+    tiles = [jnp.zeros((2 * nr, 128), F32) for _ in range(D // 128)]
+    for b in range(TP):
+        first = quarter * b // 128 * 128
+        choose = unit_mine & (unit_at + (quarter * b - first) == unit_col)
+        both = jnp.concatenate(
+            [v.PG[:, pl.ds(b * D, D)], v.PG[:, pl.ds((TP + b) * D, D)]], axis=0
+        ).astype(BF)
+        found = dot(both, jnp.where(choose, 1.0, 0.0).astype(BF))
+        for i in range(span // 128):
+            tiles[first // 128 + i] = tiles[first // 128 + i] + found[:, i * 128 : (i + 1) * 128]
+    hidden = jnp.concatenate(tiles, axis=1).astype(BF)
+    W7[4, wrow(f), :] = hidden[:nr]
+    W7[5, wrow(f), :] = hidden[nr:]
     pl.semaphore_wait(barrier, N - 1)
 
     spread("ids", ids_out.at[d], ids_out)
@@ -382,7 +417,6 @@
     for j in range(3):
         projected = dot(v.H0B[...], W7[j])
         QKV[j] = (turn(projected, 1.0) if j < 2 else projected).astype(BF)
-    length = v.length_in[0]
     allowed = lax.broadcasted_iota(jnp.int32, (1, S), 1) < length
     scaling = HD ** (-0.5)
     first_half = lax.broadcasted_iota(jnp.int32, (S, 128), 1) < HD
@@ -622,9 +656,51 @@
     def ge_down(order, origin, src, only):
         send("ed", order * NZ + origin, src, line(r, x, order, origin), (r, f - NX), only)
 
+    ry, rc, ryc = g * TP + ty, g * TP + tc, g * TP + tyc
+
+    def ge_line(order, i, only=None, src=None):
+        here = line(r, x, order, i)
+        src = here if src is None else src
+        if order == 0:
+            send("e0x", i, src, here, dev_x, only)
+            send("e0y", i * NX + x, src, here, dev_y, only)
+            send("e0c", i * NX + x, src, here, dev_c, only)
+        else:
+            send("e1y", i, src, here, dev_y, only)
+            send("e1x", i, src, here, dev_x, only)
+            send("e1c", i * NX + x, src, here, dev_c, only)
+
+    def ge_second(i, only):
+        here = line(r, 1 - x, 0, i)
+        arrive("e0x", i, here, only)
+        send("e0y", i * NX + 1 - x, here, here, dev_y, only)
+        send("e0c", i * NX + 1 - x, here, here, dev_c, only)
+        here = line(ry, x, 1, i)
+        arrive("e1y", i, here, only)
+        send("e1x", NZ + i, here, here, dev_x, only)
+        send("e1c", NF + i * NX + x, here, here, dev_c, only)
+
+    def ge_third(i, only):
+        for which_x in (x, 1 - x):
+            here = line(ry, which_x, 0, i)
+            arrive("e0y", i * NX + which_x, here, only)
+            send("e0c", NF + i * NX + which_x, here, here, dev_c, only)
+        for which, rep in enumerate((r, ry)):
+            here = line(rep, 1 - x, 1, i)
+            arrive("e1x", which * NZ + i, here, only)
+            send("e1c", which * NF + i * NX + 1 - x, here, here, dev_c, only)
+
+    def at_distance(step, k):
+        low, high = z - k, z + k
+        step(jnp.maximum(low, 0), low >= 0)
+        if k:
+            step(jnp.minimum(high, NZ - 1), high < NZ)
+
     for order in range(2):
-        ge_up(order, z, DB.at[2, :, cols[order]], z + 1 < NZ)
-        ge_down(order, z, DB.at[2, :, cols[order]], z >= 1)
+        own_cols = DB.at[2, :, cols[order]]
+        ge_up(order, z, own_cols, z + 1 < NZ)
+        ge_down(order, z, own_cols, z >= 1)
+        ge_line(order, z, None, own_cols)
 
     def ge_relay(k):
         low, high = z - k, z + k
@@ -632,8 +708,48 @@
         for order in range(2):
             arrive("eu", order * NZ + below, line(r, x, order, below), low >= 0)
             ge_up(order, below, line(r, x, order, below), (low >= 0) & (z + 1 < NZ))
+            ge_line(order, below, low >= 0)
             arrive("ed", order * NZ + above, line(r, x, order, above), high < NZ)
             ge_down(order, above, line(r, x, order, above), (high < NZ) & (z >= 1))
+            ge_line(order, above, high < NZ)
+
+    def own_lists():
+        for i in range(N):
+            v.IDF[pl.ds(i, 1), :] = ids_out[i, :, pl.ds(0, S)].astype(F32)
+            v.PM[pl.ds(i, 1), pl.ds(0, S)] = ids_out[i, :, pl.ds(S, S)].astype(F32)
+        local_row = v.IDF[...] - (f * rows).astype(F32)
+        valid = lax.broadcasted_iota(jnp.int32, (N, S), 1).astype(F32) < v.PM[:, 0:S]
+        mine = valid & (local_row >= 0.0) & (local_row < 1.0 * rows)
+        marks = jnp.where(mine, 1.0, 0.0).astype(BF)
+        before = lax.broadcasted_iota(jnp.int32, (S, S), 0) < lax.broadcasted_iota(jnp.int32, (S, S), 1)
+        prefix = dot(marks, jnp.where(before, 1.0, 0.0).astype(BF))
+        counts = jnp.zeros((N, S), F32) + jnp.sum(marks.astype(F32), axis=1, keepdims=True)
+        offsets = dot(jnp.where(row_at > col_at, 1.0, 0.0).astype(BF), counts.astype(BF))
+        place = prefix + offsets
+        high = jnp.floor(place * (1.0 / S))
+        v.RANK[0] = high
+        v.RANK[1] = jnp.where(mine, place - high * S, -1.0)
+        v.IDF[...] = jnp.where(mine, local_row, 0.0)
+        slot_at = lax.broadcasted_iota(jnp.int32, (N, S), 0).astype(F32)
+        low_at = lax.broadcasted_iota(jnp.int32, (S, S), 0).astype(F32)
+        token_at = lax.broadcasted_iota(jnp.int32, (1, S), 1).astype(F32)
+
+        def one(i, carry):
+            at = pl.ds(i, 1)
+            row = v.IDF[at, :]
+            row_high = jnp.floor(row * (1.0 / 64))
+            spot = v.RANK[0, at, :] == slot_at
+            left = jnp.concatenate(
+                [jnp.where(spot, item, 0.0) for item in (row_high, row - row_high * 64.0, token_at)], axis=0
+            ).astype(BF)
+            right = jnp.where(v.RANK[1, at, :] == low_at, 1.0, 0.0).astype(BF)
+            return carry + dot_nt(left, right)
+
+        found = lax.fori_loop(0, N, one, jnp.zeros((3 * N, S), F32))
+        v.list_out[0] = (found[:N] * 64.0 + found[N : 2 * N]).astype(jnp.int32)
+        v.list_out[1] = found[2 * N :].astype(jnp.int32)
+        v.list_out[2] = offsets.astype(jnp.int32)
+        v.list_out[3] = (offsets + counts).astype(jnp.int32)
 
     v.NGS[0] = jnp.concatenate(
         [d_gain_zero, d_shift_zero, d_gain_one, d_shift_one, d_gain_two, d_shift_two,
@@ -646,20 +762,6 @@
     def norm_add(i):
         arrive(stages[i][0], 0, v.NGR.at[i])
         v.NGS[i + 1] = v.NGS[i] + v.NGR[i]
-
-    norm_send(0)
-    pass_on(2)
-    for which in range(TP):
-        arrive("lx", which, v.LX.at[which], t != which)
-        arrive("rx", which, v.RX.at[which], t != which)
-    product(product_rows(v.LX), lambda: v.RX[...].reshape(TP * S, D), 0)
-    give(0)
-    norm_add(0)
-    norm_send(1)
-    got_own.wait()
-    ge_relay(1)
-    norm_add(1)
-    norm_send(2)
 
     def settle(m, out, at):
         for i in range(NZ):
@@ -684,60 +786,72 @@
             total = total + v.FG[k, pl.ds(first, size)].astype(F32)
         out[t] = total.astype(BF)
 
+    def share_start(name, buffer):
+        send(name, 0, buffer.at[t], buffer.at[t], dev_y)
+        send(name, 1, buffer.at[t], buffer.at[t], dev_c)
+
+    def share_pass(name, buffer):
+        arrive(name, 0, buffer.at[ty])
+        send(name, 2, buffer.at[ty], buffer.at[ty], dev_c)
+
+    def share_end(name, buffer):
+        arrive(name, 1, buffer.at[tc])
+        arrive(name, 2, buffer.at[tyc])
+
+    norm_send(0)
+    pass_on(2)
+    for which in range(TP):
+        arrive("lx", which, v.LX.at[which], t != which)
+        arrive("rx", which, v.RX.at[which], t != which)
+    product(product_rows(v.LX), lambda: v.RX[...].reshape(TP * S, D), 0)
+    give(0)
+    norm_add(0)
+    norm_send(1)
+    got_own.wait()
+    ge_relay(1)
+    at_distance(ge_second, 0)
     settle(3, v.ff_out, pl.ds(2 * nr, nr))
     settle(1, v.ff_out, pl.ds(0, nr))
+    norm_add(1)
+    norm_send(2)
+    pass_on(0)
     for k in range(2, NZ):
         ge_relay(k)
+        at_distance(ge_second, k - 1)
+    settle(2, v.ff_out, pl.ds(nr, nr))
+    if NG > 1:
+        group_sum(v.ff_out, nr, 3 * nr)
+    share_start("ff", v.ff_out)
+    at_distance(ge_second, NZ - 1)
     norm_add(2)
     for i in range(NZ):
         send("nz", i, v.NGS.at[3], v.NGZ.at[z], (r, i * NX + x), z != i, z)
         keep(z == i, v.NGZ, i, v.NGS[3])
-    for i in range(NZ):
-        here = line(r, x, 0, i)
-        send("gex", i, here, here, dev_x)
-    for i in range(NZ):
-        here = line(r, x, 1, i)
-        send("gey", i, here, here, dev_y)
-    pass_on(0)
-    settle(2, v.ff_out, pl.ds(nr, nr))
-    if NG > 1:
-        group_sum(v.ff_out, nr, 3 * nr)
     own = v.ff_out[t].astype(F32)
     squares = jnp.sum(own * own)
-    ry, rc, ryc = g * TP + ty, g * TP + tc, g * TP + tyc
-    for i in range(NZ):
-        arrive("gex", i, line(r, 1 - x, 0, i))
-    send("e1", 0, all_of(r, 0), all_of(r, 0), dev_y)
-    send("e3", 0, all_of(r, 0), all_of(r, 0), dev_c)
-    for i in range(NZ):
-        arrive("gey", i, line(ry, x, 1, i))
-    for i in range(NZ):
-        for which, rep in enumerate((r, ry)):
-            here = line(rep, x, 1, i)
-            send("gez", which * NZ + i, here, here, dev_x)
-    share("ff", v.ff_out)
     settle(0, v.fa_out, pl.ds(0, nr))
     if NG > 1:
         group_sum(v.fa_out, 0, nr)
+    share_start("fa", v.fa_out)
     own = v.fa_out[t].astype(F32)
     squares = squares + jnp.sum(own * own)
     squares = jnp.where(g == 0, squares, 0.0)
-    share("fa", v.fa_out)
-
+    own_lists()
+    for k in range(NZ):
+        at_distance(ge_third, k)
+    for name, buffer in (("ff", v.ff_out), ("fa", v.fa_out)):
+        share_pass(name, buffer)
     for i in range(NZ):
         arrive("nz", i, v.NGZ.at[i], z != i)
     total_norms = v.NGZ[0]
     for i in range(1, NZ):
         total_norms = total_norms + v.NGZ[i]
-    arrive("e1", 0, all_of(ry, 0))
-    send("e3", 1, all_of(ry, 0), all_of(ry, 0), dev_c)
-    for i in range(NZ):
-        for which, rep in enumerate((r, ry)):
-            arrive("gez", which * NZ + i, line(rep, 1 - x, 1, i))
-    send("e3", 2, all_of(r, 1), all_of(r, 1), dev_c)
-    send("e3", 3, all_of(ry, 1), all_of(ry, 1), dev_c)
-    for which, (rep, order) in enumerate(((rc, 0), (ryc, 0), (rc, 1), (ryc, 1))):
-        arrive("e3", which, all_of(rep, order))
+    for name, buffer in (("ff", v.ff_out), ("fa", v.fa_out)):
+        share_end(name, buffer)
+    for order, name in enumerate(("e0c", "e1c")):
+        for which, rep in enumerate((rc, ryc)):
+            for i in range(NF):
+                arrive(name, which * NF + i, ge_out.at[rep * NF + i, :, cols[order]])
     if NG > 1:
 
         def group(which):
@@ -805,10 +919,11 @@
             jax.ShapeDtypeStruct((TP, nr, D), BF),
             jax.ShapeDtypeStruct((8, D), F32),
             jax.ShapeDtypeStruct((8, 128), F32),
+            jax.ShapeDtypeStruct((4, N, S), jnp.int32),
             jax.ShapeDtypeStruct((N, S, D), BF),
         ),
-        in_specs=[smem] + [vmem] * 6 + [hbm] * 2,
-        out_specs=(vmem,) * 5 + (hbm,),
+        in_specs=[smem] + [vmem] * 6 + [hbm] * 5,
+        out_specs=(vmem,) * 6 + (hbm,),
         scratch_shapes=[pltpu.VMEM(*item) for item in buffers.values()]
         + [
             pltpu.SMEM((NF, 1, 2 * S), jnp.int32), pltpu.SemaphoreType.DMA((many,)),
@@ -835,16 +950,15 @@
 def finish_kernel(sizes, *refs):
     NR, NF, S, D, rows = sizes
     N, nr = NR * NF, D // NF
-    names = ("ids", "ge", "ff", "fa", "norms", "stats", "pw", "pm", "pv") + tuple(
+    names = ("lists", "ge", "ff", "fa", "norms", "stats", "pw", "pm", "pv") + tuple(
         f"{kind}{which}" for kind in "eaogd" for which in range(3)
     )
     results = ("qw", "qm", "qv") + tuple(f"{kind}{which}_new" for kind in "eaogd" for which in range(3))
     scratch = (
-        "grads", "landing", "stage", "TB", "LA", "LO", "LG", "LD", "row_of", "token_of", "first_of", "sems",
+        "grads", "landing", "stage", "TB", "LA", "LO", "LG", "LD", "sems",
         "ins", "outs", "tin", "tout",
     )
     v = types.SimpleNamespace(**dict(zip((*names, *results, *scratch), refs, strict=True)))
-    start_row = lax.axis_index("fsdp") * rows
     n_chunks = rows // CHUNK
 
     def fetch(s):
@@ -952,35 +1066,20 @@
 
     lax.fori_loop(0, n_chunks, clear, 0)
 
-    def scan(s, count):
-        v.first_of[s] = count
-
-        def eight(b, inner):
-            for i in range(8):
-                j = b * 8 + i
-                row = v.ids[s, 0, j] - start_row
-                inside = (row >= 0) & (row < rows)
-                v.row_of[inner] = row
-                v.token_of[inner] = j
-                inner = inner + inside.astype(jnp.int32)
-            return inner
-
-        return lax.fori_loop(0, lax.shift_right_logical(v.ids[s, 0, S] + 7, 3), eight, count)
-
-    v.first_of[N] = lax.fori_loop(0, N, scan, 0)
-
     def sequence(s, carry):
         pl.when(s + 3 < N)(lambda: fetch(s + 3).start())
         fetch(s).wait()
         v.stage[...] = v.landing[lax.rem(s, 4)].astype(F32)
 
         def token(k, inner):
-            at = pl.ds(v.row_of[k], 1)
-            v.grads[at, :] = v.grads[at, :] + v.stage[pl.ds(v.token_of[k], 1), :]
+            high, low = lax.shift_right_logical(k, shift), lax.bitwise_and(k, S - 1)
+            at = pl.ds(v.lists[0, high, low], 1)
+            v.grads[at, :] = v.grads[at, :] + v.stage[pl.ds(v.lists[1, high, low], 1), :]
             return inner
 
-        return lax.fori_loop(v.first_of[s], v.first_of[s + 1], token, carry)
-
+        return lax.fori_loop(v.lists[2, s, 0], v.lists[3, s, 0], token, carry)
+
+    shift = S.bit_length() - 1
     lax.fori_loop(0, N, sequence, 0)
 
     for k in range(n_chunks):
@@ -1016,7 +1115,7 @@
             item.wait()
 
 
-def finish(sizes, ids, ge, ff, fa, norms, stats, norm_state, states):
+def finish(sizes, lists, ge, ff, fa, norms, stats, norm_state, states):
     NR, NF, S, D, rows = sizes
     N, nr = NR * NF, D // NF
     hbm = pl.BlockSpec(memory_space=pl.ANY)
@@ -1035,13 +1134,12 @@
             pltpu.VMEM((SLOTS, 3, CHUNK, D), F32),
             pltpu.VMEM((3, nr, 3 * D), F32), pltpu.VMEM((3, nr, D), F32), pltpu.VMEM((3, nr, 8 * D), F32),
             pltpu.VMEM((3, 4 * nr, D), F32),
-            pltpu.SMEM((N * S + 8,), jnp.int32), pltpu.SMEM((N * S + 8,), jnp.int32),
-            pltpu.SMEM((N + 1,), jnp.int32), pltpu.SemaphoreType.DMA((4,)), pltpu.SemaphoreType.DMA((12,)),
+            pltpu.SemaphoreType.DMA((4,)), pltpu.SemaphoreType.DMA((12,)),
             pltpu.SemaphoreType.DMA((12,)), pltpu.SemaphoreType.DMA((SLOTS, 3)),
             pltpu.SemaphoreType.DMA((SLOTS, 3)),
         ],
         compiler_params=pltpu.CompilerParams(vmem_limit_bytes=62_000_000),
-    )(ids, ge, ff, fa, norms, stats, *norm_state, *flat)
+    )(lists, ge, ff, fa, norms, stats, *norm_state, *flat)
 
 
 def table_kernel(sizes, ids, ge, factor, w, m, v, w_out, m_out, v_out, grads, landing, stage, sems):
@@ -1147,29 +1245,26 @@
         * (1000.0 ** (-2.0 * jnp.arange(HD // 2).astype(F32) / HD))[None, :]
     )
     cosine, sine = jnp.tile(jnp.cos(angles), (1, 128 * 2 // HD)), jnp.tile(jnp.sin(angles), (1, 128 * 2 // HD))
-    attention = jnp.concatenate(
-        [attend_weight.reshape(nr, 3, D).transpose(1, 0, 2), attention_output_matrix[None]], axis=0
-    ).astype(BF)
-    hidden = gate_up.astype(BF).reshape(nr, 2, NF, TP, nr).transpose(3, 1, 0, 2, 4).reshape(TP, 2, nr, D)
-    down = contract_kernel.astype(BF).reshape(TP, 1, nr, D)
-    pieces = jnp.concatenate([attention[:, None], hidden, down], axis=1)
-    ids, ffn, att, norms, stats, ge = run_step(
+    ids, ffn, att, norms, stats, lists, ge = run_step(
         sizes,
         lengths,
-        jnp.concatenate([token_ids, jnp.broadcast_to(lengths[:, None], (1, S))], axis=1),
+        token_ids,
         norm_params,
         slot_order.reshape(1, N),
         pair_labels.reshape(1, N),
         cosine,
         sine,
-        pieces,
+        attend_weight,
+        attention_output_matrix,
+        gate_up,
+        contract_kernel,
         embedding,
     )
     loss_value, grad_norm = stats[0, 0], stats[1, 0]
     if rows % CHUNK == 0:
         norm_next, *rest = split_three(
             finish(
-                sizes, ids, ge, ffn, att, norms, stats, (norm_params, norm_first, norm_second),
+                sizes, lists, ge, ffn, att, norms, stats, (norm_params, norm_first, norm_second),
                 (
                     (embedding, embedding_first, embedding_second),
                     (attend_weight, attend_first, attend_second),

time: 338 us -> 291 us (0.86)
  Pallas kernels: 323 us -> 286 us
  other arithmetic: 5 us -> 0.15 us
  local copies, waits for them, and re-layouts: 7.27 us -> 2.75 us
    pallas_call x1, Pallas kernels: 263 us -> 238 us  [run_step(): pl.pallas_call(functools.partial(step_kernel, sizes), name='step', out_sh...]
    pallas_call x1, Pallas kernels: 59.8 us -> 48.1 us  [finish(): pl.pallas_call(functools.partial(finish_kernel, sizes), name='finish', ou...]
where the time goes in v3:
time: 291 us; the launch traced here: 290 us
  Pallas kernels  286 us (98%)
    pallas_call x1, Pallas kernels, run_step(): pl.pallas_call(functools.partial(step_kernel, sizes), name='step', out_sh...  238 us
    pallas_call x1, Pallas kernels, finish(): pl.pallas_call(functools.partial(finish_kernel, sizes), name='finish', ou...  48.1 us

profile of v3, /device:TPU:0, one launch (start us, length us, event | category | flops | bytes accessed | tf_op | source)
XLA Modules:
  0.0 290.1 jit_solution(11246332642415047071)
XLA Ops:
  0.7 0.1 multiply_sine_fusion
  0.8 0.7 copy.42.refs_5_
  1.6 0.7 copy.43.refs_6_
  3.0 237.7 %step.1 = (s32[32,1,256]{2,1,0:T(1,128)}, bf16[4,288,768]{2,1,0:T(8,128)(2,1)}, bf16[4,96,768]{2,1,0:T(8,128)(2,1)}, f32[8,768]{1,0:T(8,128)}, f32[8,128]{1,0:T(...) custom-call(s32[1]{0:T(128)S(6)} %copy.44.refs_0_, s32[1,128]{1,0:T(1,128)} %refs_1_.1, f32[6,96]{1,0:T(8,128)} %refs_6_.1, ...), custom_call_target="tpu_custom_call" | custom-call | tf_op jit(solution)/shard_map/step/pallas_call | solution.py:913
  240.7 48.1 %finish.1 = (f32[6,96]{1,0:T(8,128)}, f32[6,96]{1,0:T(8,128)}, f32[6,96]{1,0:T(8,128)}, f32[3816,768]{1,0:T(8,128)}, f32[3816,768]{1,0:T(8,128)}, /*index=5*/f32...) custom-call(s32[4,32,128]{2,1,0:T(8,128)} %get-tuple-element.45.refs, ...), custom_call_target="tpu_custom_call" | custom-call | tf_op jit(solution)/shard_map/finish/pallas_call | solution.py:1126
  288.8 1.3 fusion
  (4 shorter events, 0.0 us)

commit v4 on v3

--- a/solution.py
+++ b/solution.py
@@ -351,7 +351,7 @@
             arrive("wx3", z, piece(3, z, 1 - x))
             up_to(3, z, z + 1 < NZ, 1 - x)
             down_to(3, z, z >= 1, 1 - x)
-        while at_step < len(steps) * (number + 1) // (len(jobs) + 2) - 1:
+        while at_step < len(steps) * (number + 1) // len(jobs):
             relay(*steps[at_step])
             at_step += 1
 
@@ -641,7 +641,7 @@
     DB[2] = d_embedded.astype(BF)
 
     got_own = load(DB.at[2], ge_out.at[d], 0)
-    cut = D * 2 // 3
+    cut = D // 2
     cols = [pl.ds(0, cut), pl.ds(cut, D - cut)]
 
     def line(rep, which_x, order, i):
@@ -814,14 +814,14 @@
     settle(1, v.ff_out, pl.ds(0, nr))
     norm_add(1)
     norm_send(2)
+    settle(2, v.ff_out, pl.ds(nr, nr))
+    if NG > 1:
+        group_sum(v.ff_out, nr, 3 * nr)
+    share_start("ff", v.ff_out)
     pass_on(0)
     for k in range(2, NZ):
         ge_relay(k)
         at_distance(ge_second, k - 1)
-    settle(2, v.ff_out, pl.ds(nr, nr))
-    if NG > 1:
-        group_sum(v.ff_out, nr, 3 * nr)
-    share_start("ff", v.ff_out)
     at_distance(ge_second, NZ - 1)
     norm_add(2)
     for i in range(NZ):
@@ -944,7 +944,7 @@
     return (weight - rate * (update + weight_decay * weight), first_new, second_new)
 
 
-CHUNK, SLOTS = 424, 6
+CHUNK, SLOTS = 424, 7
 
 
 def finish_kernel(sizes, *refs):

time: 291 us -> 279 us (0.959)
  Pallas kernels: 286 us -> 274 us
    pallas_call x1, Pallas kernels: 238 us -> 228 us  [run_step(): pl.pallas_call(functools.partial(step_kernel, sizes), name='step', out_sh...]
where the time goes in v4:
time: 279 us; the launch traced here: 278 us
  Pallas kernels  274 us (98%)
    pallas_call x1, Pallas kernels, run_step(): pl.pallas_call(functools.partial(step_kernel, sizes), name='step', out_sh...  228 us
    pallas_call x1, Pallas kernels, finish(): pl.pallas_call(functools.partial(finish_kernel, sizes), name='finish', ou...  46.4 us

profile of v4, /device:TPU:0, one launch (start us, length us, event | category | flops | bytes accessed | tf_op | source)
XLA Modules:
  0.0 278.4 jit_solution(2099804214595436645)
XLA Ops:
  0.7 0.1 multiply_sine_fusion
  0.8 0.7 copy.42.refs_5_
  1.6 0.7 copy.43.refs_6_
  3.0 227.8 %step.1 = (s32[32,1,256]{2,1,0:T(1,128)}, bf16[4,288,768]{2,1,0:T(8,128)(2,1)}, bf16[4,96,768]{2,1,0:T(8,128)(2,1)}, f32[8,768]{1,0:T(8,128)}, f32[8,128]{1,0:T(...) custom-call(s32[1]{0:T(128)S(6)} %copy.44.refs_0_, s32[1,128]{1,0:T(1,128)} %refs_1_.1, f32[6,96]{1,0:T(8,128)} %refs_6_.1, ...), custom_call_target="tpu_custom_call" | custom-call | tf_op jit(solution)/shard_map/step/pallas_call | solution.py:913
  230.7 46.4 %finish.1 = (f32[6,96]{1,0:T(8,128)}, f32[6,96]{1,0:T(8,128)}, f32[6,96]{1,0:T(8,128)}, f32[3816,768]{1,0:T(8,128)}, f32[3816,768]{1,0:T(8,128)}, /*index=5*/f32...) custom-call(s32[4,32,128]{2,1,0:T(8,128)} %get-tuple-element.45.refs, ...), custom_call_target="tpu_custom_call" | custom-call | tf_op jit(solution)/shard_map/finish/pallas_call | solution.py:1126
  277.1 1.3 fusion
  (4 shorter events, 0.0 us)

commit v5 on v4

--- a/solution.py
+++ b/solution.py
@@ -397,8 +397,6 @@
         send(name, which, src, buffer.at[t], (g * TP + which, f), t != which, t)
         keep(t == which, buffer, which, src[...])
 
-    for which in range(3):
-        to_rank("lx", which, v.H0B, v.LX)
 
     for i in range(NF):
         arrive("ac", i, W7.at[tc, wrow(i)])
@@ -468,7 +466,6 @@
         return mine + v.YR[which].astype(F32)
 
     share("h1", v.H1)
-    to_rank("lx", 3, v.ATT, v.LX)
     for m in range(1, 3):
         for i in range(NZ):
             arrive(f"wx{m}", i, piece(m, i, 1 - x))
@@ -484,6 +481,9 @@
 
     lax.fori_loop(0, TP, forward, 0)
     feed = reduce(("fc", "fy"), PT, CR, 0)
+    for which in range(3):
+        to_rank("lx", which, v.H0B, v.LX)
+    to_rank("lx", 3, v.ATT, v.LX)
     normed, hat, inverse = layer_norm(pool[blk(H1F), :] + feed, gain[4], gain[5])
     pool[blk(HAT, 2), :] = hat
     v.INV[2] = inverse

time: 279 us -> 277 us (level)
  no operation moved by 1% of the time
where the time goes in v5:
time: 277 us; the launch traced here: 276 us
  Pallas kernels  272 us (98%)
    pallas_call x1, Pallas kernels, run_step(): pl.pallas_call(functools.partial(step_kernel, sizes), name='step', out_sh...  226 us
    pallas_call x1, Pallas kernels, finish(): pl.pallas_call(functools.partial(finish_kernel, sizes), name='finish', ou...  46.3 us

profile of v5, /device:TPU:0, one launch (start us, length us, event | category | flops | bytes accessed | tf_op | source)
XLA Modules:
  0.0 276.4 jit_solution(641193915072553081)
XLA Ops:
  0.7 0.1 multiply_sine_fusion
  0.8 0.7 copy.42.refs_5_
  1.6 0.7 copy.43.refs_6_
  3.0 225.9 %step.1 = (s32[32,1,256]{2,1,0:T(1,128)}, bf16[4,288,768]{2,1,0:T(8,128)(2,1)}, bf16[4,96,768]{2,1,0:T(8,128)(2,1)}, f32[8,768]{1,0:T(8,128)}, f32[8,128]{1,0:T(...) custom-call(s32[1]{0:T(128)S(6)} %copy.44.refs_0_, s32[1,128]{1,0:T(1,128)} %refs_1_.1, f32[6,96]{1,0:T(8,128)} %refs_6_.1, ...), custom_call_target="tpu_custom_call" | custom-call | tf_op jit(solution)/shard_map/step/pallas_call | solution.py:913
  228.8 46.3 %finish.1 = (f32[6,96]{1,0:T(8,128)}, f32[6,96]{1,0:T(8,128)}, f32[6,96]{1,0:T(8,128)}, f32[3816,768]{1,0:T(8,128)}, f32[3816,768]{1,0:T(8,128)}, /*index=5*/f32...) custom-call(s32[4,32,128]{2,1,0:T(8,128)} %get-tuple-element.45.refs, ...), custom_call_target="tpu_custom_call" | custom-call | tf_op jit(solution)/shard_map/finish/pallas_call | solution.py:1126
  275.2 1.3 fusion
  (4 shorter events, 0.0 us)

commit v6 on v5

--- a/solution.py
+++ b/solution.py
@@ -493,13 +493,53 @@
 
     spread("pool", v.PROW.at[0], v.PB)
     v.PB[d] = v.PROW[0]
+    row_at = lax.broadcasted_iota(jnp.int32, (N, N), 0)
+    col_at = lax.broadcasted_iota(jnp.int32, (N, N), 1)
+
+    def own_lists():
+        for i in range(N):
+            v.IDF[pl.ds(i, 1), :] = ids_out[i, :, pl.ds(0, S)].astype(F32)
+            v.PM[pl.ds(i, 1), pl.ds(0, S)] = ids_out[i, :, pl.ds(S, S)].astype(F32)
+        local_row = v.IDF[...] - (f * rows).astype(F32)
+        valid = lax.broadcasted_iota(jnp.int32, (N, S), 1).astype(F32) < v.PM[:, 0:S]
+        mine = valid & (local_row >= 0.0) & (local_row < 1.0 * rows)
+        marks = jnp.where(mine, 1.0, 0.0).astype(BF)
+        before = lax.broadcasted_iota(jnp.int32, (S, S), 0) < lax.broadcasted_iota(jnp.int32, (S, S), 1)
+        prefix = dot(marks, jnp.where(before, 1.0, 0.0).astype(BF))
+        counts = jnp.zeros((N, S), F32) + jnp.sum(marks.astype(F32), axis=1, keepdims=True)
+        offsets = dot(jnp.where(row_at > col_at, 1.0, 0.0).astype(BF), counts.astype(BF))
+        place = prefix + offsets
+        high = jnp.floor(place * (1.0 / S))
+        v.RANK[0] = high
+        v.RANK[1] = jnp.where(mine, place - high * S, -1.0)
+        v.IDF[...] = jnp.where(mine, local_row, 0.0)
+        slot_at = lax.broadcasted_iota(jnp.int32, (N, S), 0).astype(F32)
+        low_at = lax.broadcasted_iota(jnp.int32, (S, S), 0).astype(F32)
+        token_at = lax.broadcasted_iota(jnp.int32, (1, S), 1).astype(F32)
+
+        def one(i, carry):
+            at = pl.ds(i, 1)
+            row = v.IDF[at, :]
+            row_high = jnp.floor(row * (1.0 / 64))
+            spot = v.RANK[0, at, :] == slot_at
+            left = jnp.concatenate(
+                [jnp.where(spot, item, 0.0) for item in (row_high, row - row_high * 64.0, token_at)], axis=0
+            ).astype(BF)
+            right = jnp.where(v.RANK[1, at, :] == low_at, 1.0, 0.0).astype(BF)
+            return carry + dot_nt(left, right)
+
+        found = lax.fori_loop(0, N, one, jnp.zeros((3 * N, S), F32))
+        v.list_out[0] = (found[:N] * 64.0 + found[N : 2 * N]).astype(jnp.int32)
+        v.list_out[1] = found[2 * N :].astype(jnp.int32)
+        v.list_out[2] = offsets.astype(jnp.int32)
+        v.list_out[3] = (offsets + counts).astype(jnp.int32)
+
+    own_lists()
     gather_all("pool", v.PB)
     for i in range(N):
         v.PM[pl.ds(i, 1), :] = v.PB[i]
     pooled = v.PM[...]
     wide = lax.broadcasted_iota(jnp.int32, (N, D), 1)
-    row_at = lax.broadcasted_iota(jnp.int32, (N, N), 0)
-    col_at = lax.broadcasted_iota(jnp.int32, (N, N), 1)
     order, labels = v.order_in[...].astype(F32), v.labels_in[...].astype(F32)
 
     def column(row):
@@ -712,44 +752,6 @@
             arrive("ed", order * NZ + above, line(r, x, order, above), high < NZ)
             ge_down(order, above, line(r, x, order, above), (high < NZ) & (z >= 1))
             ge_line(order, above, high < NZ)
-
-    def own_lists():
-        for i in range(N):
-            v.IDF[pl.ds(i, 1), :] = ids_out[i, :, pl.ds(0, S)].astype(F32)
-            v.PM[pl.ds(i, 1), pl.ds(0, S)] = ids_out[i, :, pl.ds(S, S)].astype(F32)
-        local_row = v.IDF[...] - (f * rows).astype(F32)
-        valid = lax.broadcasted_iota(jnp.int32, (N, S), 1).astype(F32) < v.PM[:, 0:S]
-        mine = valid & (local_row >= 0.0) & (local_row < 1.0 * rows)
-        marks = jnp.where(mine, 1.0, 0.0).astype(BF)
-        before = lax.broadcasted_iota(jnp.int32, (S, S), 0) < lax.broadcasted_iota(jnp.int32, (S, S), 1)
-        prefix = dot(marks, jnp.where(before, 1.0, 0.0).astype(BF))
-        counts = jnp.zeros((N, S), F32) + jnp.sum(marks.astype(F32), axis=1, keepdims=True)
-        offsets = dot(jnp.where(row_at > col_at, 1.0, 0.0).astype(BF), counts.astype(BF))
-        place = prefix + offsets
-        high = jnp.floor(place * (1.0 / S))
-        v.RANK[0] = high
-        v.RANK[1] = jnp.where(mine, place - high * S, -1.0)
-        v.IDF[...] = jnp.where(mine, local_row, 0.0)
-        slot_at = lax.broadcasted_iota(jnp.int32, (N, S), 0).astype(F32)
-        low_at = lax.broadcasted_iota(jnp.int32, (S, S), 0).astype(F32)
-        token_at = lax.broadcasted_iota(jnp.int32, (1, S), 1).astype(F32)
-
-        def one(i, carry):
-            at = pl.ds(i, 1)
-            row = v.IDF[at, :]
-            row_high = jnp.floor(row * (1.0 / 64))
-            spot = v.RANK[0, at, :] == slot_at
-            left = jnp.concatenate(
-                [jnp.where(spot, item, 0.0) for item in (row_high, row - row_high * 64.0, token_at)], axis=0
-            ).astype(BF)
-            right = jnp.where(v.RANK[1, at, :] == low_at, 1.0, 0.0).astype(BF)
-            return carry + dot_nt(left, right)
-
-        found = lax.fori_loop(0, N, one, jnp.zeros((3 * N, S), F32))
-        v.list_out[0] = (found[:N] * 64.0 + found[N : 2 * N]).astype(jnp.int32)
-        v.list_out[1] = found[2 * N :].astype(jnp.int32)
-        v.list_out[2] = offsets.astype(jnp.int32)
-        v.list_out[3] = (offsets + counts).astype(jnp.int32)
 
     v.NGS[0] = jnp.concatenate(
         [d_gain_zero, d_shift_zero, d_gain_one, d_shift_one, d_gain_two, d_shift_two,
@@ -836,7 +838,6 @@
     own = v.fa_out[t].astype(F32)
     squares = squares + jnp.sum(own * own)
     squares = jnp.where(g == 0, squares, 0.0)
-    own_lists()
     for k in range(NZ):
         at_distance(ge_third, k)
     for name, buffer in (("ff", v.ff_out), ("fa", v.fa_out)):

time: 277 us -> 275 us (level)
  no operation moved by 1% of the time
where the time goes in v6:
time: 275 us; the launch traced here: 274 us
  Pallas kernels  270 us (98%)
  local copies, waits for them, and re-layouts  2.75 us (1%)
    pallas_call x1, Pallas kernels, run_step(): pl.pallas_call(functools.partial(step_kernel, sizes), name='step', out_sh...  224 us
    pallas_call x1, Pallas kernels, finish(): pl.pallas_call(functools.partial(finish_kernel, sizes), name='finish', ou...  46.3 us

profile of v6, /device:TPU:0, one launch (start us, length us, event | category | flops | bytes accessed | tf_op | source)
XLA Modules:
  0.0 274.3 jit_solution(2772654347269418608)
XLA Ops:
  0.7 0.1 multiply_sine_fusion
  0.8 0.7 copy.42.refs_5_
  1.6 0.7 copy.43.refs_6_
  3.0 223.8 %step.1 = (s32[32,1,256]{2,1,0:T(1,128)}, bf16[4,288,768]{2,1,0:T(8,128)(2,1)}, bf16[4,96,768]{2,1,0:T(8,128)(2,1)}, f32[8,768]{1,0:T(8,128)}, f32[8,128]{1,0:T(...) custom-call(s32[1]{0:T(128)S(6)} %copy.44.refs_0_, s32[1,128]{1,0:T(1,128)} %refs_1_.1, f32[6,96]{1,0:T(8,128)} %refs_6_.1, ...), custom_call_target="tpu_custom_call" | custom-call | tf_op jit(solution)/shard_map/step/pallas_call | solution.py:914
  226.7 46.3 %finish.1 = (f32[6,96]{1,0:T(8,128)}, f32[6,96]{1,0:T(8,128)}, f32[6,96]{1,0:T(8,128)}, f32[3816,768]{1,0:T(8,128)}, f32[3816,768]{1,0:T(8,128)}, /*index=5*/f32...) custom-call(s32[4,32,128]{2,1,0:T(8,128)} %get-tuple-element.45.refs, ...), custom_call_target="tpu_custom_call" | custom-call | tf_op jit(solution)/shard_map/finish/pallas_call | solution.py:1127
  273.0 1.3 fusion
  (4 shorter events, 0.0 us)
